TPU v7x, 32 devices: a whole 2x2x4 slice. The times are simulated.
32 devices in a mesh: tile: 8 (over y, x, core), grp: 4 (over z).
Axes of the slice: x: 2, y: 2, z: 4, core: 2. Of those that a mesh axis runs over, the one named last changes fastest.
Arguments:
- earlier_flow_speeds: float32 [2, 64, 256, 512], P(None, None, 'tile', 'grp'), may hold values from -6 to 6
- flow_rate_factor: float32 [64, 256, 512], P(None, 'tile', 'grp'), may hold values from 0.5 to 2
- scaled_warmth: float32 [64, 256, 512], P('grp', 'tile'), may hold values from -3 to 3
- gravity_forcing: float32 [2, 256, 512], P(None, 'tile', 'grp'), may hold values from -6 to 6
- sliding_coefficient: float32 [256, 512], P('tile', 'grp'), may hold values from 1 to 10
- icy_column_flag: int32 [256, 512], P('tile', 'grp'), may hold values 0 or 1
- resting_on_bed_flag: int32 [256, 512], P('tile', 'grp'), may hold values 0 or 1
Outputs:
- velocity: float32 [2, 64, 256, 512], P(None, None, 'tile', 'grp')
- temperature_next: float32 [64, 256, 512], P('grp', 'tile')
- hardness_next: float32 [64, 256, 512], P(None, 'tile', 'grp')
All inputs are finite; a program needn't handle non-finite values. No bound on the sum of `icy_column_flag` or of `resting_on_bed_flag` on one device may be relied on, other than what follows from the above.
Results may differ from a plain program's by a relative error of at most 0.00002.
Values sent between devices are 32-bit elements; how exact they have to be, the bound alone decides.
A program may use at most 64 MiB of HBM per device.

v0:
```python
import jax
import jax.numpy as jnp
from jax import lax
from jax.sharding import PartitionSpec as P

SWEEPS = 4
SECTIONS = 4


vertical_weight = 4.0
strain_floor = 0.01
cross_weight = 0.75
diag_weight = 22.0
diffuse_flat = 0.1
diffuse_vert = 0.2
advect_weight = 0.05
heat_weight = 0.05
arrhenius = 0.6


def with_halo(block, sides, width):
    for axis, dim in sides:
        count = lax.axis_size(axis)
        forward = [(i, i + 1) for i in range(count - 1)]
        backward = [(target, source) for source, target in forward]
        low = lax.ppermute(
            lax.slice_in_dim(block, block.shape[dim] - width, None, axis=dim), axis, forward
        )
        high = lax.ppermute(lax.slice_in_dim(block, 0, width, axis=dim), axis, backward)
        block = jnp.concatenate([low, block, high], axis=dim)
    return block


def level_pad(field):
    return jnp.concatenate([field[:1], field, field[-1:]], axis=0)


def strain_parts(padded_u, padded_v):
    center_u = padded_u[:, 1:-1, 1:-1]
    center_v = padded_v[:, 1:-1, 1:-1]
    strain_xx = 0.5 * (padded_u[:, 2:, 1:-1] - padded_u[:, :-2, 1:-1])
    shear_uy = 0.5 * (padded_u[:, 1:-1, 2:] - padded_u[:, 1:-1, :-2])
    shear_vx = 0.5 * (padded_v[:, 2:, 1:-1] - padded_v[:, :-2, 1:-1])
    strain_yy = 0.5 * (padded_v[:, 1:-1, 2:] - padded_v[:, 1:-1, :-2])
    column_u = level_pad(center_u)
    column_v = level_pad(center_v)
    vert_u = 0.5 * (column_u[2:] - column_u[:-2])
    vert_v = 0.5 * (column_v[2:] - column_v[:-2])
    shear = shear_uy + shear_vx
    effective = (
        strain_xx * strain_xx
        + strain_yy * strain_yy
        + strain_xx * strain_yy
        + 0.25 * shear * shear
        + 0.25 * (vert_u * vert_u + vert_v * vert_v)
    )
    return (effective, column_u, column_v)


def viscosity_of(flow_rate_factor, effective):
    return flow_rate_factor * jnp.power(effective + strain_floor, -1.0 / 3.0)


def jacobi_sweep(
    padded_u, padded_v, flow_rate_factor, drive_u, driving_stress_north, drag_base, ice
):
    effective, column_u, column_v = strain_parts(padded_u, padded_v)
    viscosity = viscosity_of(flow_rate_factor, effective)
    levels = padded_u.shape[0]
    bottom = (lax.broadcasted_iota(jnp.int32, (levels, 1, 1), 0) == 0).astype(jnp.float32)
    diagonal = viscosity * diag_weight + bottom * drag_base[None]
    near_u = (
        4.0 * (padded_u[:, 2:, 1:-1] + padded_u[:, :-2, 1:-1])
        + (padded_u[:, 1:-1, 2:] + padded_u[:, 1:-1, :-2])
        + vertical_weight * (column_u[2:] + column_u[:-2])
    )
    near_v = (
        padded_v[:, 2:, 1:-1]
        + padded_v[:, :-2, 1:-1]
        + 4.0 * (padded_v[:, 1:-1, 2:] + padded_v[:, 1:-1, :-2])
        + vertical_weight * (column_v[2:] + column_v[:-2])
    )
    cross_u = cross_weight * (
        padded_v[:, 2:, 2:] - padded_v[:, :-2, 2:] - padded_v[:, 2:, :-2] + padded_v[:, :-2, :-2]
    )
    cross_v = cross_weight * (
        padded_u[:, 2:, 2:] - padded_u[:, :-2, 2:] - padded_u[:, 2:, :-2] + padded_u[:, :-2, :-2]
    )
    guard = diagonal + (1.0 - ice[None])
    new_u = ice[None] * (drive_u[None] + viscosity * (near_u + cross_u)) / guard
    new_v = ice[None] * (driving_stress_north[None] + viscosity * (near_v + cross_v)) / guard
    return jnp.stack([new_u, new_v])


def heating(padded_u, padded_v, flow_rate_factor, ice):
    effective, column_u, column_v = strain_parts(padded_u, padded_v)
    return ice[None] * 2.0 * viscosity_of(flow_rate_factor, effective) * effective


def thermal_section(padded, speed_u, speed_v, heat):
    center = padded[1:-1, 1:-1, 1:-1]
    east = padded[1:-1, 2:, 1:-1]
    west = padded[1:-1, :-2, 1:-1]
    north = padded[1:-1, 1:-1, 2:]
    south = padded[1:-1, 1:-1, :-2]
    upper = padded[2:, 1:-1, 1:-1]
    lower = padded[:-2, 1:-1, 1:-1]
    advect = (
        jnp.maximum(speed_u, 0.0) * (center - west)
        + jnp.minimum(speed_u, 0.0) * (east - center)
        + jnp.maximum(speed_v, 0.0) * (center - south)
        + jnp.minimum(speed_v, 0.0) * (north - center)
    )
    return (
        center
        + diffuse_flat * (east + west + north + south - 4.0 * center)
        + diffuse_vert * (upper + lower - 2.0 * center)
        - advect_weight * advect
        + heat_weight * heat
    )


def trim(field, width):
    rows = field.shape[-2]
    cols = field.shape[-1]
    return field[..., width : rows - width, width : cols - width]


def local(
    earlier_flow_speeds,
    flow_rate_factor,
    scaled_warmth,
    gravity_forcing,
    sliding_coefficient,
    icy_column_flag,
    resting_on_bed_flag,
):
    ice = icy_column_flag.astype(jnp.float32)
    drag_base = sliding_coefficient * resting_on_bed_flag.astype(jnp.float32)
    width = SWEEPS + 1
    stacked = with_halo(
        jnp.concatenate([earlier_flow_speeds, flow_rate_factor[None]], 0),
        (("tile", 2), ("grp", 3)),
        width,
    )
    columns = with_halo(
        jnp.stack([gravity_forcing[0], gravity_forcing[1], drag_base, ice]),
        (("tile", 1), ("grp", 2)),
        width,
    )
    moving = stacked[:2]
    for sweep in range(SWEEPS):
        inner = sweep + 1
        static = trim(columns, inner)
        moving = jacobi_sweep(
            moving[0],
            moving[1],
            trim(stacked[2], inner),
            static[0],
            static[1],
            static[2],
            static[3],
        )
    heat = heating(moving[0], moving[1], trim(stacked[2], width), ice)
    current = trim(moving, 1)
    moved = lax.all_to_all(
        jnp.concatenate([current, heat[None]], 0), "grp", split_axis=1, concat_axis=3, tiled=True
    )
    heat_content_field = scaled_warmth
    for section in range(SECTIONS):
        padded = with_halo(heat_content_field, (("tile", 1), ("grp", 0)), 1)
        padded = jnp.pad(padded, ((0, 0), (0, 0), (1, 1)))
        heat_content_field = thermal_section(padded, moved[0], moved[1], moved[2])
    hardness_next = lax.all_to_all(
        jnp.exp(-arrhenius * heat_content_field), "grp", split_axis=2, concat_axis=0, tiled=True
    )
    return (current, heat_content_field, hardness_next)


def solution(mesh):
    return jax.shard_map(
        local,
        mesh=mesh,
        in_specs=(
            P(None, None, "tile", "grp"),
            P(None, "tile", "grp"),
            P("grp", "tile", None),
            P(None, "tile", "grp"),
            P("tile", "grp"),
            P("tile", "grp"),
            P("tile", "grp"),
        ),
        out_specs=(P(None, None, "tile", "grp"), P("grp", "tile", None), P(None, "tile", "grp")),
        check_vma=False,
    )
```

profile of v0, /device:TPU:2, one launch (start us, length us, event | category | flops | bytes accessed | tf_op | source)
XLA Modules:
  0.0 373.7 jit_solution(10286295420754703820)
XLA Ops:
  0.6 2.9 copy.155
  6.2 3.6 collective-permute-start.5
  11.9 3.6 collective-permute-start.1
  16.1 2.9 collective-permute-done.1
  19.2 3.5 collective-permute-start.2
  25.0 4.7 %collective-permute-done.3 = f32[4,42,5]{2,1,0:T(8,128)S(1)} collective-permute-done((f32[4,42,5]{2,1,0:T(8,128)S(1)}, f32[4,42,5]{2,1,0:T(8,128)S(1)}, u32[]{:S(2)}, u32[]{:S(2)}) %collective-permute-start.3) | collective-permute-done | bytes 3392 | tf_op jit(solution)/shard_map/ppermute | solution.py:29
  34.0 5.0 %fusion.145 = (f32[3,64,42,5]{3,1,2,0:T(8,128)}, f32[3,64,42,5]{3,1,2,0:T(8,128)}) fusion(f32[3,64,42,128]{3,1,2,0:T(8,128)S(1)} %pad_maximum_fusion.1), kind=kLoop, calls=%fused_computation.309 | loop fusion | bytes 645120 | tf_op jit(solution)/shard_map/slice | solution.py:27
  39.0 3.9 %copy.156 = f32[3,64,42,5]{1,2,3,0:T(8,128)} copy(f32[3,64,42,5]{3,1,2,0:T(8,128)} %get-tuple-element.28) | data formatting | bytes 322560 | tf_op jit(solution)/shard_map/slice | solution.py:27
  42.9 4.2 %collective-permute-start.6 = (f32[3,64,42,5]{1,2,3,0:T(8,128)}, f32[3,64,42,5]{1,2,3,0:T(8,128)}, u32[]{:S(2)}, u32[]{:S(2)}) collective-permute-start(f32[3,64,42,5]{1,2,3,0:T(8,128)} %copy.156), channel_id=1, source_target_pairs={{0,1},{1,2},{2,3},{4,5},{5,6},{6,7},{8,9},{9,10},{10,11},{12,13},{... | collective-permute-start | bytes 483848 | tf_op jit(solution)/shard_map/ppermute | solution.py:26
  47.1 3.9 %copy.157 = f32[3,64,42,5]{1,2,3,0:T(8,128)} copy(f32[3,64,42,5]{3,1,2,0:T(8,128)} %get-tuple-element.29) | data formatting | bytes 322560 | tf_op jit(solution)/shard_map/slice | solution.py:29
  55.0 3.7 copy.158
  58.7 5.1 %collective-permute-done.7 = f32[3,64,42,5]{1,2,3,0:T(8,128)} collective-permute-done((f32[3,64,42,5]{1,2,3,0:T(8,128)}, f32[3,64,42,5]{1,2,3,0:T(8,128)}, u32[]{:S(2)}, u32[]{:S(2)}) %collective-permute-start.7) | collective-permute-done | bytes 161312 | tf_op jit(solution)/shard_map/ppermute | solution.py:29
  63.8 3.7 copy.159
  67.5 7.9 %pad_maximum_fusion = f32[3,64,42,138]{3,1,2,0:T(8,128)S(1)} fusion(f32[3,64,42,5]{3,1,2,0:T(8,128)} %copy.159, f32[3,64,5,128]{3,1,2,0:T(8,128)} %copy-done.9, f32[1,64,32,128]{3,1,2,0:T(8,128)S(1)} %bitcast.73, f32[2,64,32,128]{3,1,2,0:T(8,128)S(1)} %copy.155, f32[3,64,5,128]{3,1,2,0:T(8,128)} %copy-done.8, f32[3,64,42,5]{3,1,2,0:T(8,128)} %copy.158), kind=kLoop, calls=%fused_computation | loop fusion | flops 5564160 | bytes 8902656 | tf_op jit(solution)/shard_map/concatenate | solution.py:30
  78.5 10.8 %fusion.11 = (f32[64,40,136]{2,0,1:T(8,128)S(1)}, f32[64,40,136]{2,0,1:T(8,128)}) fusion(f32[64,42,138]{2,0,1:T(8,128)S(1)} %get-tuple-element.26, f32[64,42,138]{2,0,1:T(8,128)S(1)} %get-tuple-element.27, f32[1,40,136]{2,0,1:T(1,128)S(1)} %get-tuple-element.97, f32[64,40,136]{2,0,1:T(8,128)S(1)} %slice.1001, f32[1,40,136]{2,0,1:T(1,128)S(1)} %get-tuple-element.98, ...), kind=kLoop, calls=%fused_computation.24 | loop fusion | flops 17756160 | bytes 23849216 | tf_op jit(solution)/shard_map/div | solution.py:90
  89.3 5.7 %fusion.5 = f32[64,40,136]{2,0,1:T(8,128)S(1)} fusion(f32[64,40,136]{2,0,1:T(8,128)} %get-tuple-element.24, f32[64,42,138]{2,0,1:T(8,128)S(1)} %get-tuple-element.27, f32[64,42,138]{2,0,1:T(8,128)S(1)} %get-tuple-element.26, f32[1,40,136]{2,0,1:T(1,128)S(1)} %get-tuple-element.37, f32[64,40,136]{2,0,1:T(8,128)S(1)} %slice.1004, ...), kind=kLoop, calls=%fused_computation.15 | loop fusion | flops 7659520 | bytes 15449856 | tf_op jit(solution)/shard_map/div | solution.py:91
  99.9 14.6 %fusion.23 = (f32[64,38,134]{2,0,1:T(8,128)S(1)}, f32[64,38,134]{2,0,1:T(8,128)}) fusion(f32[64,40,136]{2,0,1:T(8,128)S(1)} %fusion.5, f32[64,40,136]{2,0,1:T(8,128)S(1)} %get-tuple-element.23, f32[1,38,134]{2,0,1:T(1,128)S(1)} %get-tuple-element.44, f32[64,38,134]{2,0,1:T(8,128)} %slice.1025, f32[1,38,134]{2,0,1:T(1,128)S(1)} %get-tuple-element.43, ...), kind=kLoop, calls=%fused_computation.48 | loop fusion | flops 16620288 | bytes 22323584 | tf_op jit(solution)/shard_map/div | solution.py:90
  114.5 7.5 %fusion.17 = f32[64,38,134]{2,0,1:T(8,128)S(1)} fusion(f32[64,38,134]{2,0,1:T(8,128)} %get-tuple-element.22, f32[64,40,136]{2,0,1:T(8,128)S(1)} %get-tuple-element.23, f32[64,40,136]{2,0,1:T(8,128)S(1)} %fusion.5, f32[1,38,134]{2,0,1:T(1,128)S(1)} %get-tuple-element.41, f32[64,38,134]{2,0,1:T(8,128)} %slice.1028, f32[1,38,134]{2,0,1:T(1,128)S(1)} %get-tuple-element.42, ...), kind=kLoop, calls=%fused_computation.39 | loop fusion | flops 7169536 | bytes 14461536 | tf_op jit(solution)/shard_map/div | solution.py:91
  124.7 8.9 %fusion.35 = (f32[64,36,132]{2,0,1:T(8,128)S(1)}, f32[64,36,132]{2,0,1:T(8,128)S(1)}) fusion(f32[64,38,134]{2,0,1:T(8,128)S(1)} %fusion.17, f32[64,38,134]{2,0,1:T(8,128)S(1)} %get-tuple-element.21, f32[1,36,132]{2,0,1:T(1,128)S(1)} %get-tuple-element.48, f32[64,36,132]{2,0,1:T(8,128)S(1)} %slice.1049, f32[1,36,132]{2,0,1:T(1,128)S(1)} %get-tuple-element.47, ...), kind=kLoop, calls=%fused_computation.72 | loop fusion | flops 15510528 | bytes 20833024 | tf_op jit(solution)/shard_map/div | solution.py:90
  133.6 4.6 %fusion.29 = f32[64,36,132]{2,0,1:T(8,128)S(1)} fusion(f32[64,36,132]{2,0,1:T(8,128)S(1)} %get-tuple-element.20, f32[64,38,134]{2,0,1:T(8,128)S(1)} %get-tuple-element.21, f32[64,38,134]{2,0,1:T(8,128)S(1)} %fusion.17, f32[1,36,132]{2,0,1:T(1,128)S(1)} %get-tuple-element.45, f32[64,36,132]{2,0,1:T(8,128)S(1)} %slice.1052, ...), kind=kLoop, calls=%fused_computation.63 | loop fusion | flops 6690816 | bytes 13495936 | tf_op jit(solution)/shard_map/div | solution.py:91
  141.4 11.9 %fusion.47 = (f32[64,34,130]{2,0,1:T(8,128)S(1)}, f32[64,34,130]{2,0,1:T(8,128)}) fusion(f32[64,36,132]{2,0,1:T(8,128)S(1)} %fusion.29, f32[64,36,132]{2,0,1:T(8,128)S(1)} %get-tuple-element.19, f32[1,34,130]{2,0,1:T(1,128)S(1)} %get-tuple-element.52, f32[64,34,130]{2,0,1:T(8,128)} %slice.1073, f32[1,34,130]{2,0,1:T(1,128)S(1)} %get-tuple-element.51, ...), kind=kLoop, calls=%fused_computation.96 | loop fusion | flops 14426880 | bytes 19377536 | tf_op jit(solution)/shard_map/div | solution.py:90
  153.3 6.9 %fusion.41 = f32[64,34,130]{2,0,1:T(8,128)S(1)} fusion(f32[64,34,130]{2,0,1:T(8,128)} %get-tuple-element.18, f32[64,36,132]{2,0,1:T(8,128)S(1)} %get-tuple-element.19, f32[64,36,132]{2,0,1:T(8,128)S(1)} %fusion.29, f32[1,34,130]{2,0,1:T(1,128)S(1)} %get-tuple-element.49, f32[64,34,130]{2,0,1:T(8,128)} %copy-done.4, f32[1,34,130]{2,0,1:T(1,128)S(1)} %get-tuple-element.50, ...), kind=kLoop, calls=%fused_computation.87 | loop fusion | flops 6223360 | bytes 12553056 | tf_op jit(solution)/shard_map/div | solution.py:91
  161.9 3.2 fusion.123
  165.3 3.5 copy.166
  168.8 3.7 all-to-all-start
  178.1 2.8 collective-permute-done.9
  181.8 3.9 %collective-permute-start.10 = (f32[1,34,512]{2,1,0:T(8,128)S(1)}, f32[1,34,512]{2,1,0:T(8,128)S(1)}, u32[]{:S(2)}, u32[]{:S(2)}) collective-permute-start(f32[1,34,512]{2,1,0:T(8,128)S(1)} %get-tuple-element.64), channel_id=1, source_target_pairs={{0,1},{1,2},{2,3},{4,5},{5,6},{6,7},{8,9},{9,10},{10,11},{12,13},{... | collective-permute-start | bytes 208904 | tf_op jit(solution)/shard_map/ppermute | solution.py:26
  187.2 37.4 %collective-permute-done.10 = f32[1,34,512]{2,1,0:T(8,128)S(1)} collective-permute-done((f32[1,34,512]{2,1,0:T(8,128)S(1)}, f32[1,34,512]{2,1,0:T(8,128)S(1)}, u32[]{:S(2)}, u32[]{:S(2)}) %collective-permute-start.10) | collective-permute-done | bytes 69664 | tf_op jit(solution)/shard_map/ppermute | solution.py:26
  226.7 17.0 %all-to-all-done = f32[3,64,32,128]{3,2,0,1:T(8,128)S(1)} async-done(((f32[3,64,32,128]{3,2,0,1:T(8,128)}), f32[3,64,32,128]{3,2,0,1:T(8,128)S(1)}, u32[]{:S(2)}, u32[]{:S(2)}) %all-to-all-start) | async-done | bytes 3145760 | tf_op jit(solution)/shard_map/all_to_all | solution.py:166
  243.6 2.9 copy.193
  246.5 3.0 slice_maximum_fusion
  252.0 2.6 min.21
  257.2 5.4 %fusion.129 = f32[16,32,512]{2,1,0:T(8,128)S(1)} fusion(f32[16,32,512]{2,1,0:T(8,128)} %mul.776, f32[1,34,512]{2,1,0:T(8,128)S(1)} %collective-permute-done.10, f32[16,1,512]{2,1,0:T(1,128)S(1)} %copy.161, f32[16,32,512]{2,1,0:T(8,128)} %param.9, f32[16,1,512]{2,1,0:T(1,128)S(1)} %copy.163, f32[1,34,512]{2,1,0:T(8,128)S(1)} %collective-permute-done.11, ...), kind=kLoop, calls=%fused_computation.238 | loop fusion | flops 8912896 | bytes 9641984 | tf_op jit(solution)/shard_map/add | solution.py:115
  267.3 2.8 collective-permute-done.13
  270.1 5.4 %collective-permute-start.14 = (f32[1,34,512]{2,1,0:T(8,128)S(1)}, f32[1,34,512]{2,1,0:T(8,128)S(1)}, u32[]{:S(2)}, u32[]{:S(2)}) collective-permute-start(f32[1,34,512]{2,1,0:T(8,128)S(1)} %get-tuple-element.62), channel_id=1, source_target_pairs={{0,1},{1,2},{2,3},{4,5},{5,6},{6,7},{8,9},{9,10},{10,11},{12,13},{... | collective-permute-start | bytes 208904 | tf_op jit(solution)/shard_map/ppermute | solution.py:26
  277.6 4.3 %collective-permute-done.15 = f32[1,34,512]{2,1,0:T(8,128)S(1)} collective-permute-done((f32[1,34,512]{2,1,0:T(8,128)S(1)}, f32[1,34,512]{2,1,0:T(8,128)S(1)}, u32[]{:S(2)}, u32[]{:S(2)}) %collective-permute-start.15) | collective-permute-done | bytes 69664 | tf_op jit(solution)/shard_map/ppermute | solution.py:29
  289.2 2.8 collective-permute-done.17
  296.6 4.3 %collective-permute-done.19 = f32[1,34,512]{2,1,0:T(8,128)S(1)} collective-permute-done((f32[1,34,512]{2,1,0:T(8,128)S(1)}, f32[1,34,512]{2,1,0:T(8,128)S(1)}, u32[]{:S(2)}, u32[]{:S(2)}) %collective-permute-start.19) | collective-permute-done | bytes 69664 | tf_op jit(solution)/shard_map/ppermute | solution.py:29
  308.2 2.8 collective-permute-done.21
  315.2 4.1 %collective-permute-done.23 = f32[1,34,512]{2,1,0:T(8,128)S(1)} collective-permute-done((f32[1,34,512]{2,1,0:T(8,128)S(1)}, f32[1,34,512]{2,1,0:T(8,128)S(1)}, u32[]{:S(2)}, u32[]{:S(2)}) %collective-permute-start.23) | collective-permute-done | bytes 69664 | tf_op jit(solution)/shard_map/ppermute | solution.py:29
  320.1 3.1 multiply_exponential_fusion
  323.2 4.7 %copy.186 = f32[16,32,512]{1,0,2:T(8,128)} copy(f32[16,32,512]{2,1,0:T(8,128)} %get-tuple-element.15) | data formatting | bytes 2097152 | tf_op jit(solution)/shard_map/exp | solution.py:175
  327.9 4.8 %reshape.31 = f32[4,1,65536]{2,1,0:T(1,128)} reshape(f32[512,16,32]{2,1,0:T(8,128)} %bitcast.69) | data formatting | bytes 2097152
  332.7 3.6 all-to-all-start.1
  338.9 22.8 %all-to-all-done.1 = f32[4,1,65536]{2,1,0:T(1,128)S(1)} async-done(((f32[4,1,65536]{2,1,0:T(1,128)}), f32[4,1,65536]{2,1,0:T(1,128)S(1)}, u32[]{:S(2)}, u32[]{:S(2)}) %all-to-all-start.1) | async-done | bytes 1048608 | tf_op jit(solution)/shard_map/all_to_all | solution.py:174
  362.3 3.7 reduce
  366.0 3.5 reshape.32
  369.5 3.8 %copy.187 = f32[4,16,32,128]{3,2,1,0:T(8,128)} copy(f32[4,16,32,128]{2,1,3,0:T(8,128)} %bitcast.70) | data formatting | bytes 2097152 | tf_op jit(solution)/shard_map/all_to_all | solution.py:174
  (166 shorter events, 80.3 us)
Async XLA Ops:
  0.6 2.9 copy-start.10
  4.2 5.7 %copy-start.28 = (s32[32,128]{1,0:T(8,128)S(1)}, s32[32,128]{1,0:T(8,128)}, u32[]{:S(2)}) copy-start(s32[32,128]{1,0:T(8,128)} %param.12) | copy-start | bytes 49156
  4.2 5.7 %copy-start.29 = (f32[32,128]{1,0:T(8,128)S(1)}, f32[32,128]{1,0:T(8,128)}, u32[]{:S(2)}) copy-start(f32[32,128]{1,0:T(8,128)} %param.11) | copy-start | bytes 49156
  4.2 5.7 %copy-start.30 = (s32[32,128]{1,0:T(8,128)S(1)}, s32[32,128]{1,0:T(8,128)}, u32[]{:S(2)}) copy-start(s32[32,128]{1,0:T(8,128)} %param.13) | copy-start | bytes 49156
  4.2 5.7 %copy-start.18 = (f32[2,32,128]{2,1,0:T(8,128)S(1)}, f32[2,32,128]{2,1,0:T(8,128)}, u32[]{:S(2)}) copy-start(f32[2,32,128]{2,1,0:T(8,128)} %param.10) | copy-start | bytes 98308
  4.3 27.9 %collective-permute-start.4 = (f32[3,64,5,128]{3,1,2,0:T(8,128)S(1)}, f32[3,64,5,128]{3,1,2,0:T(8,128)S(1)}, u32[]{:S(2)}, u32[]{:S(2)}) collective-permute-start(f32[3,64,5,128]{3,1,2,0:T(8,128)S(1)} %get-tuple-element.35), channel_id=1, source_target_pairs={{0,4},{4,8},{8,12},{12,16},{16,20},{20,24},{24,28},{1,5},{5,9},{9,... | collective-permute-start | bytes 1474568 | tf_op jit(solution)/shard_map/ppermute | solution.py:26
  6.2 25.9 %collective-permute-start.5 = (f32[3,64,5,128]{3,1,2,0:T(8,128)S(1)}, f32[3,64,5,128]{3,1,2,0:T(8,128)S(1)}, u32[]{:S(2)}, u32[]{:S(2)}) collective-permute-start(f32[3,64,5,128]{3,1,2,0:T(8,128)S(1)} %get-tuple-element.36), channel_id=1, source_target_pairs={{4,0},{8,4},{12,8},{16,12},{20,16},{24,20},{28,24},{5,1},{9,5},{13... | collective-permute-start | bytes 1474568 | tf_op jit(solution)/shard_map/ppermute | solution.py:29
  9.9 6.2 %collective-permute-start = (f32[4,5,128]{2,1,0:T(8,128)S(1)}, f32[4,5,128]{2,1,0:T(8,128)S(1)}, u32[]{:S(2)}, u32[]{:S(2)}) collective-permute-start(f32[4,5,128]{2,1,0:T(8,128)S(1)} %get-tuple-element.95), channel_id=1, source_target_pairs={{0,4},{4,8},{8,12},{12,16},{16,20},{20,24},{24,28},{1,5},{5,9},{9,... | collective-permute-start | bytes 30728 | tf_op jit(solution)/shard_map/ppermute | solution.py:26
  11.9 7.2 %collective-permute-start.1 = (f32[4,5,128]{2,1,0:T(8,128)S(1)}, f32[4,5,128]{2,1,0:T(8,128)S(1)}, u32[]{:S(2)}, u32[]{:S(2)}) collective-permute-start(f32[4,5,128]{2,1,0:T(8,128)S(1)} %get-tuple-element.96), channel_id=1, source_target_pairs={{4,0},{8,4},{12,8},{16,12},{20,16},{24,20},{28,24},{5,1},{9,5},{13... | collective-permute-start | bytes 30728 | tf_op jit(solution)/shard_map/ppermute | solution.py:29
  19.2 5.9 %collective-permute-start.2 = (f32[4,42,5]{2,1,0:T(8,128)S(1)}, f32[4,42,5]{2,1,0:T(8,128)S(1)}, u32[]{:S(2)}, u32[]{:S(2)}) collective-permute-start(f32[4,42,5]{2,1,0:T(8,128)S(1)} %get-tuple-element.93), channel_id=1, source_target_pairs={{0,1},{1,2},{2,3},{4,5},{5,6},{6,7},{8,9},{9,10},{10,11},{12,13},{... | collective-permute-start | bytes 10088 | tf_op jit(solution)/shard_map/ppermute | solution.py:26
  22.7 7.0 %collective-permute-start.3 = (f32[4,42,5]{2,1,0:T(8,128)S(1)}, f32[4,42,5]{2,1,0:T(8,128)S(1)}, u32[]{:S(2)}, u32[]{:S(2)}) collective-permute-start(f32[4,42,5]{2,1,0:T(8,128)S(1)} %get-tuple-element.94), channel_id=1, source_target_pairs={{1,0},{2,1},{3,2},{5,4},{6,5},{7,6},{9,8},{10,9},{11,10},{13,12},{... | collective-permute-start | bytes 10088 | tf_op jit(solution)/shard_map/ppermute | solution.py:29
  42.9 12.1 %collective-permute-start.6 = (f32[3,64,42,5]{1,2,3,0:T(8,128)}, f32[3,64,42,5]{1,2,3,0:T(8,128)}, u32[]{:S(2)}, u32[]{:S(2)}) collective-permute-start(f32[3,64,42,5]{1,2,3,0:T(8,128)} %copy.156), channel_id=1, source_target_pairs={{0,1},{1,2},{2,3},{4,5},{5,6},{6,7},{8,9},{9,10},{10,11},{12,13},{... | collective-permute-start | bytes 483848 | tf_op jit(solution)/shard_map/ppermute | solution.py:26
  51.0 12.8 %collective-permute-start.7 = (f32[3,64,42,5]{1,2,3,0:T(8,128)}, f32[3,64,42,5]{1,2,3,0:T(8,128)}, u32[]{:S(2)}, u32[]{:S(2)}) collective-permute-start(f32[3,64,42,5]{1,2,3,0:T(8,128)} %copy.157), channel_id=1, source_target_pairs={{1,0},{2,1},{3,2},{5,4},{6,5},{7,6},{9,8},{10,9},{11,10},{13,12},{... | collective-permute-start | bytes 483848 | tf_op jit(solution)/shard_map/ppermute | solution.py:29
  76.5 1.9 copy-start
  78.5 10.8 %copy-start.25 = (f32[40,136]{1,0:T(8,128)S(1)}, f32[40,136]{1,0:T(8,128)}, u32[]{:S(2)}) copy-start(f32[40,136]{1,0:T(8,128)} %get-tuple-element.88) | copy-start | bytes 65284
  97.4 2.4 copy-start.19
  99.9 14.6 %copy-start.24 = (f32[38,134]{1,0:T(8,128)S(1)}, f32[38,134]{1,0:T(8,128)}, u32[]{:S(2)}) copy-start(f32[38,134]{1,0:T(8,128)} %get-tuple-element.83) | copy-start | bytes 61108
  122.9 1.8 copy-start.1
  124.7 8.9 %copy-start.20 = (f32[36,132]{1,0:T(8,128)S(1)}, f32[36,132]{1,0:T(8,128)}, u32[]{:S(2)}) copy-start(f32[36,132]{1,0:T(8,128)} %get-tuple-element.78) | copy-start | bytes 57028
  138.8 2.5 copy-start.4
  138.8 2.5 copy-start.12
  138.8 2.5 copy-start.13
  138.9 2.5 copy-start.14
  138.9 2.5 copy-start.23
  141.4 12.0 %copy-start.21 = (f32[34,130]{1,0:T(8,128)S(1)}, f32[34,130]{1,0:T(8,128)}, u32[]{:S(2)}) copy-start(f32[34,130]{1,0:T(8,128)} %get-tuple-element.73) | copy-start | bytes 53044
  161.8 3.3 copy-start.5
  168.8 74.9 %all-to-all-start = ((f32[3,64,32,128]{3,2,0,1:T(8,128)}), f32[3,64,32,128]{3,2,0,1:T(8,128)S(1)}, u32[]{:S(2)}, u32[]{:S(2)}) async-start(f32[3,64,32,128]{3,2,0,1:T(8,128)} %copy.166), calls=%async_computation | async-start | bytes 6291456 | tf_op jit(solution)/shard_map/all_to_all | solution.py:166
  172.5 52.1 %copy-start.7 = (f32[16,32,512]{2,1,0:T(8,128)S(1)}, f32[16,32,512]{2,1,0:T(8,128)}, u32[]{:S(2)}) copy-start(f32[16,32,512]{2,1,0:T(8,128)} %param.9) | copy-start | bytes 3145732
  173.7 4.4 %collective-permute-start.8 = (f32[16,1,512]{2,0,1:T(8,128)S(1)}, f32[16,1,512]{2,0,1:T(8,128)S(1)}, u32[]{:S(2)}, u32[]{:S(2)}) collective-permute-start(f32[16,1,512]{2,0,1:T(8,128)S(1)} %copy.189), channel_id=1, source_target_pairs={{4,0},{8,4},{12,8},{16,12},{20,16},{24,20},{28,24},{5,1},{9,5},{13... | collective-permute-start | bytes 98312 | tf_op jit(solution)/shard_map/ppermute | solution.py:29
  175.6 5.2 %collective-permute-start.9 = (f32[16,1,512]{2,0,1:T(8,128)S(1)}, f32[16,1,512]{2,0,1:T(8,128)S(1)}, u32[]{:S(2)}, u32[]{:S(2)}) collective-permute-start(f32[16,1,512]{2,0,1:T(8,128)S(1)} %copy.190), channel_id=1, source_target_pairs={{0,4},{4,8},{8,12},{12,16},{16,20},{20,24},{24,28},{1,5},{5,9},{9,... | collective-permute-start | bytes 98312 | tf_op jit(solution)/shard_map/ppermute | solution.py:26
  181.8 42.8 %collective-permute-start.10 = (f32[1,34,512]{2,1,0:T(8,128)S(1)}, f32[1,34,512]{2,1,0:T(8,128)S(1)}, u32[]{:S(2)}, u32[]{:S(2)}) collective-permute-start(f32[1,34,512]{2,1,0:T(8,128)S(1)} %get-tuple-element.64), channel_id=1, source_target_pairs={{0,1},{1,2},{2,3},{4,5},{5,6},{6,7},{8,9},{9,10},{10,11},{12,13},{... | collective-permute-start | bytes 208904 | tf_op jit(solution)/shard_map/ppermute | solution.py:26
  185.7 38.9 %collective-permute-start.11 = (f32[1,34,512]{2,1,0:T(8,128)S(1)}, f32[1,34,512]{2,1,0:T(8,128)S(1)}, u32[]{:S(2)}, u32[]{:S(2)}) collective-permute-start(f32[1,34,512]{2,1,0:T(8,128)S(1)} %get-tuple-element.63), channel_id=1, source_target_pairs={{1,0},{2,1},{3,2},{5,4},{6,5},{7,6},{9,8},{10,9},{11,10},{13,12},{... | collective-permute-start | bytes 208904 | tf_op jit(solution)/shard_map/ppermute | solution.py:29
  262.7 20.0 %copy-start.2 = (f32[16,32,512]{2,1,0:T(8,128)S(1)}, f32[16,32,512]{2,1,0:T(8,128)}, u32[]{:S(2)}) copy-start(f32[16,32,512]{2,1,0:T(8,128)} %min.21) | copy-start | bytes 3145732
  262.7 20.0 %copy-start.3 = (f32[16,32,512]{2,1,0:T(8,128)S(1)}, f32[16,32,512]{2,1,0:T(8,128)}, u32[]{:S(2)}) copy-start(f32[16,32,512]{2,1,0:T(8,128)} %mul.776) | copy-start | bytes 3145732
  262.7 4.5 %collective-permute-start.12 = (f32[16,1,512]{2,0,1:T(8,128)S(1)}, f32[16,1,512]{2,0,1:T(8,128)S(1)}, u32[]{:S(2)}, u32[]{:S(2)}) collective-permute-start(f32[16,1,512]{2,0,1:T(8,128)S(1)} %copy.168), channel_id=1, source_target_pairs={{4,0},{8,4},{12,8},{16,12},{20,16},{24,20},{28,24},{5,1},{9,5},{13... | collective-permute-start | bytes 98312 | tf_op jit(solution)/shard_map/ppermute | solution.py:29
  264.8 5.2 %collective-permute-start.13 = (f32[16,1,512]{2,0,1:T(8,128)S(1)}, f32[16,1,512]{2,0,1:T(8,128)S(1)}, u32[]{:S(2)}, u32[]{:S(2)}) collective-permute-start(f32[16,1,512]{2,0,1:T(8,128)S(1)} %copy.170), channel_id=1, source_target_pairs={{0,4},{4,8},{8,12},{12,16},{16,20},{20,24},{24,28},{1,5},{5,9},{9,... | collective-permute-start | bytes 98312 | tf_op jit(solution)/shard_map/ppermute | solution.py:26
  270.1 7.4 %collective-permute-start.14 = (f32[1,34,512]{2,1,0:T(8,128)S(1)}, f32[1,34,512]{2,1,0:T(8,128)S(1)}, u32[]{:S(2)}, u32[]{:S(2)}) collective-permute-start(f32[1,34,512]{2,1,0:T(8,128)S(1)} %get-tuple-element.62), channel_id=1, source_target_pairs={{0,1},{1,2},{2,3},{4,5},{5,6},{6,7},{8,9},{9,10},{10,11},{12,13},{... | collective-permute-start | bytes 208904 | tf_op jit(solution)/shard_map/ppermute | solution.py:26
  275.5 6.3 %collective-permute-start.15 = (f32[1,34,512]{2,1,0:T(8,128)S(1)}, f32[1,34,512]{2,1,0:T(8,128)S(1)}, u32[]{:S(2)}, u32[]{:S(2)}) collective-permute-start(f32[1,34,512]{2,1,0:T(8,128)S(1)} %get-tuple-element.61), channel_id=1, source_target_pairs={{1,0},{2,1},{3,2},{5,4},{6,5},{7,6},{9,8},{10,9},{11,10},{13,12},{... | collective-permute-start | bytes 208904 | tf_op jit(solution)/shard_map/ppermute | solution.py:29
  284.8 4.4 %collective-permute-start.16 = (f32[16,1,512]{2,0,1:T(8,128)S(1)}, f32[16,1,512]{2,0,1:T(8,128)S(1)}, u32[]{:S(2)}, u32[]{:S(2)}) collective-permute-start(f32[16,1,512]{2,0,1:T(8,128)S(1)} %copy.174), channel_id=1, source_target_pairs={{4,0},{8,4},{12,8},{16,12},{20,16},{24,20},{28,24},{5,1},{9,5},{13... | collective-permute-start | bytes 98312 | tf_op jit(solution)/shard_map/ppermute | solution.py:29
  286.7 5.2 %collective-permute-start.17 = (f32[16,1,512]{2,0,1:T(8,128)S(1)}, f32[16,1,512]{2,0,1:T(8,128)S(1)}, u32[]{:S(2)}, u32[]{:S(2)}) collective-permute-start(f32[16,1,512]{2,0,1:T(8,128)S(1)} %copy.176), channel_id=1, source_target_pairs={{0,4},{4,8},{8,12},{12,16},{16,20},{20,24},{24,28},{1,5},{5,9},{9,... | collective-permute-start | bytes 98312 | tf_op jit(solution)/shard_map/ppermute | solution.py:26
  292.0 4.5 %collective-permute-start.18 = (f32[1,34,512]{2,1,0:T(8,128)S(1)}, f32[1,34,512]{2,1,0:T(8,128)S(1)}, u32[]{:S(2)}, u32[]{:S(2)}) collective-permute-start(f32[1,34,512]{2,1,0:T(8,128)S(1)} %get-tuple-element.60), channel_id=1, source_target_pairs={{0,1},{1,2},{2,3},{4,5},{5,6},{6,7},{8,9},{9,10},{10,11},{12,13},{... | collective-permute-start | bytes 208904 | tf_op jit(solution)/shard_map/ppermute | solution.py:26
  294.5 6.3 %collective-permute-start.19 = (f32[1,34,512]{2,1,0:T(8,128)S(1)}, f32[1,34,512]{2,1,0:T(8,128)S(1)}, u32[]{:S(2)}, u32[]{:S(2)}) collective-permute-start(f32[1,34,512]{2,1,0:T(8,128)S(1)} %get-tuple-element.59), channel_id=1, source_target_pairs={{1,0},{2,1},{3,2},{5,4},{6,5},{7,6},{9,8},{10,9},{11,10},{13,12},{... | collective-permute-start | bytes 208904 | tf_op jit(solution)/shard_map/ppermute | solution.py:29
  303.8 4.4 %collective-permute-start.20 = (f32[16,1,512]{2,0,1:T(8,128)S(1)}, f32[16,1,512]{2,0,1:T(8,128)S(1)}, u32[]{:S(2)}, u32[]{:S(2)}) collective-permute-start(f32[16,1,512]{2,0,1:T(8,128)S(1)} %copy.180), channel_id=1, source_target_pairs={{4,0},{8,4},{12,8},{16,12},{20,16},{24,20},{28,24},{5,1},{9,5},{13... | collective-permute-start | bytes 98312 | tf_op jit(solution)/shard_map/ppermute | solution.py:29
  305.7 5.2 %collective-permute-start.21 = (f32[16,1,512]{2,0,1:T(8,128)S(1)}, f32[16,1,512]{2,0,1:T(8,128)S(1)}, u32[]{:S(2)}, u32[]{:S(2)}) collective-permute-start(f32[16,1,512]{2,0,1:T(8,128)S(1)} %copy.182), channel_id=1, source_target_pairs={{0,4},{4,8},{8,12},{12,16},{16,20},{20,24},{24,28},{1,5},{5,9},{9,... | collective-permute-start | bytes 98312 | tf_op jit(solution)/shard_map/ppermute | solution.py:26
  311.0 4.2 %collective-permute-start.22 = (f32[1,34,512]{2,1,0:T(8,128)S(1)}, f32[1,34,512]{2,1,0:T(8,128)S(1)}, u32[]{:S(2)}, u32[]{:S(2)}) collective-permute-start(f32[1,34,512]{2,1,0:T(8,128)S(1)} %get-tuple-element.58), channel_id=1, source_target_pairs={{0,1},{1,2},{2,3},{4,5},{5,6},{6,7},{8,9},{9,10},{10,11},{12,13},{... | collective-permute-start | bytes 208904 | tf_op jit(solution)/shard_map/ppermute | solution.py:26
  313.0 6.3 %collective-permute-start.23 = (f32[1,34,512]{2,1,0:T(8,128)S(1)}, f32[1,34,512]{2,1,0:T(8,128)S(1)}, u32[]{:S(2)}, u32[]{:S(2)}) collective-permute-start(f32[1,34,512]{2,1,0:T(8,128)S(1)} %get-tuple-element.57), channel_id=1, source_target_pairs={{1,0},{2,1},{3,2},{5,4},{6,5},{7,6},{9,8},{10,9},{11,10},{13,12},{... | collective-permute-start | bytes 208904 | tf_op jit(solution)/shard_map/ppermute | solution.py:29
  332.7 3.7 copy-start.6
  332.7 29.0 %all-to-all-start.1 = ((f32[4,1,65536]{2,1,0:T(1,128)}), f32[4,1,65536]{2,1,0:T(1,128)S(1)}, u32[]{:S(2)}, u32[]{:S(2)}) async-start(f32[4,1,65536]{2,1,0:T(1,128)} %reshape.31), calls=%async_computation.1 | async-start | bytes 2097152 | tf_op jit(solution)/shard_map/all_to_all | solution.py:174
  (9 other events, 9.0 us)
where the time goes:
time: 380 us; the launch traced here: 374 us
  waiting for transfers between devices  119 us (31%)
  other arithmetic  112 us (29%)
  local copies, waits for them, and re-layouts  75.5 us (20%)
  starting transfers between devices  65.7 us (17%)
    ppermute x12, waiting for transfers between devices, with_halo(): lax.ppermute(lax.slice_in_dim(block, block.shape[dim] - width, None, axis...  53.4 us
    div x4, other arithmetic, jacobi_sweep(): new_u = ice[None] * (drive_u[None] + viscosity * (near_u + cross_u)) / guard  46.3 us
    ppermute x12, starting transfers between devices, with_halo(): lax.ppermute(lax.slice_in_dim(block, block.shape[dim] - width, None, axis...  34.9 us
    ppermute x12, waiting for transfers between devices, with_halo(): lax.ppermute(lax.slice_in_dim(block, 0, width, axis=dim), axis, backward)  25.4 us
    div x4, other arithmetic, jacobi_sweep(): ice[None] * (driving_stress_north[None] + viscosity * (near_v + cross_v))  24.7 us
    ppermute x12, starting transfers between devices, with_halo(): lax.ppermute(lax.slice_in_dim(block, 0, width, axis=dim), axis, backward)  23.5 us
    all_to_all x1, waiting for transfers between devices, local(): lax.all_to_all(jnp.exp(-arrhenius * heat_content_field), 'grp', split_axi...  22.8 us
    unnamed x69, local copies, waits for them, and re-layouts  17 us
  transfers between devices with their start and end apart: 26, of which 18 were waited for; matrix products, arithmetic and copies ran while one was open for 5% of the time, Pallas kernels for 0%

commit v1 on v0

v1 whole, which is shorter than its diff:
```python
import functools

import jax
import jax.numpy as jnp
from jax import lax
from jax.experimental import pallas as pl
from jax.experimental.pallas import tpu as pltpu
from jax.sharding import PartitionSpec as P

SWEEPS = 4
SECTIONS = 4
LANES = 128
SUB = 8
PAD = 8

MESH = pl.DeviceIdType.MESH


def roll(x, shift, axis=1):
    return pltpu.roll(x, shift, axis)


def kernel(
    n,
    m,
    R,
    L,
    LG,
    vel_in,
    rate_in,
    warm_in,
    grav,
    slide,
    icy,
    bed,
    vel_out,
    temp_out,
    hard_out,
    vel_st,
    rate_st,
    warm_st,
    hard_st,
    U,
    DY,
    SY,
    T,
    Q,
    pk,
    dk,
    row_rx,
    col_rx,
    diag_rx,
    tpk,
    trow_rx,
    tcol_rx,
    loc_sem,
    vs_sem,
    vr_sem,
    ts_sem,
    tr_sem,
    ws_sem,
    wr_sem,
    os_sem,
    or_sem,
):
    t = lax.axis_index("tile")
    g = lax.axis_index("grp")
    LB = L // SUB
    f32 = jnp.float32

    vel_cp = [
        pltpu.make_async_copy(vel_in.at[f], vel_st.at[f], loc_sem.at[f]) for f in range(2)
    ]
    rate_cp = pltpu.make_async_copy(rate_in, rate_st, loc_sem.at[2])
    for cp in vel_cp:
        cp.start()
    rate_cp.start()

    lo_t, hi_t, lo_g, hi_g = t > 0, t < n - 1, g > 0, g < m - 1

    def has(dt, dg):
        ok = None
        for d, lo, hi in ((dt, lo_t, hi_t), (dg, lo_g, hi_g)):
            if d:
                c = lo if d < 0 else hi
                ok = c if ok is None else jnp.logical_and(ok, c)
        return ok

    for ref in (row_rx, col_rx, diag_rx, trow_rx, tcol_rx):
        ref[...] = jnp.zeros_like(ref)

    barrier = pltpu.get_barrier_semaphore()
    around = [(-1, -1), (-1, 0), (-1, 1), (1, -1), (1, 0), (1, 1)]
    for dt, dg in around:

        @pl.when(has(dt, dg))
        def _(dt=dt, dg=dg):
            pl.semaphore_signal(
                barrier, inc=1, device_id=(t + dt, g + dg), device_id_type=MESH
            )

    for d in range(1, m):
        pl.semaphore_signal(
            barrier, inc=1, device_id=(t, lax.rem(g + d, m)), device_id_type=MESH
        )

    sides_t = lo_t.astype(jnp.int32) + hi_t.astype(jnp.int32)
    sides_g = lo_g.astype(jnp.int32) + hi_g.astype(jnp.int32)
    pl.semaphore_wait(barrier, m - 1 + sides_t * (1 + sides_g))

    def warm_copy(d):
        to = lax.rem(g + d, m)
        src = warm_in.at[:, :, pl.ds(pl.multiple_of(to * LANES, LANES), LANES)]
        dst = warm_st.at[pl.ds(g * LG, LG)]
        if d == 0:
            return pltpu.make_async_copy(src, dst, loc_sem.at[3])
        return pltpu.make_async_remote_copy(
            src, dst, ws_sem.at[d], wr_sem.at[d], device_id=(t, to), device_id_type=MESH
        )

    lane = lax.broadcasted_iota(jnp.int32, (SUB, LANES), 1)
    subl = lax.broadcasted_iota(jnp.int32, (SUB, LANES), 0)
    first = lane == 0
    last = lane == LANES - 1
    odd = lax.rem(lane, 2) == 1
    half = LANES // 2
    u_edge = jnp.logical_or(first, last)

    def back(x, extra=0):
        return lax.rem(2 * LANES - 2 * x - extra, LANES)

    def near_lane(x, shift):
        lane_x = lax.rem(lane + (LANES + 1) - shift, LANES)
        return lane_x < 2

    def vel_moves(k):
        slot = k % 2
        moves = [
            ((1, 0), U.at[slot, :, R, PAD : PAD + L, :], row_rx.at[k, 0]),
            ((-1, 0), U.at[slot, :, 1, PAD : PAD + L, :], row_rx.at[k, 1]),
            ((0, 1), pk.at[k], col_rx.at[k, 0]),
            ((0, -1), pk.at[k], col_rx.at[k, 1]),
        ]
        if k < SWEEPS:
            moves += [
                ((1, 1), dk.at[k, 1], diag_rx.at[k, 0, 0]),
                ((1, -1), dk.at[k, 1], diag_rx.at[k, 0, 1]),
                ((-1, 1), dk.at[k, 0], diag_rx.at[k, 1, 0]),
                ((-1, -1), dk.at[k, 0], diag_rx.at[k, 1, 1]),
            ]
        return moves

    def start(moves, s_sem, r_sem):
        for j, ((dt, dg), src, dst) in enumerate(moves):

            @pl.when(has(dt, dg))
            def _(j=j, dt=dt, dg=dg, src=src, dst=dst):
                pltpu.make_async_remote_copy(
                    src,
                    dst,
                    s_sem.at[j],
                    r_sem.at[j],
                    device_id=(t + dt, g + dg),
                    device_id_type=MESH,
                ).start()

    def finish(moves, s_sem, r_sem):
        for j, ((dt, dg), src, dst) in enumerate(moves):

            @pl.when(has(dt, dg))
            def _(j=j, dt=dt, dg=dg, src=src, dst=dst):
                pltpu.make_async_remote_copy(
                    src,
                    dst,
                    s_sem.at[j],
                    r_sem.at[j],
                    device_id=(t + dt, g + dg),
                    device_id_type=MESH,
                ).wait_send()

            @pl.when(has(-dt, -dg))
            def _(j=j, dt=dt, dg=dg, src=src, dst=dst):
                pltpu.make_async_remote_copy(
                    src,
                    dst,
                    s_sem.at[j],
                    r_sem.at[j],
                    device_id=(t - dt, g - dg),
                    device_id_type=MESH,
                ).wait_recv()

    def put_vel(slot, k, x, b, values):
        lv = PAD + b * SUB
        for f in range(2):
            U[slot, f, x + 1, lv : lv + SUB, :] = values[f]
            if b == 0:
                U[slot, f, x + 1, lv - 1 : lv, :] = values[f][0:1]
            if b == LB - 1:
                U[slot, f, x + 1, lv + SUB : lv + SUB + 1, :] = values[f][SUB - 1 : SUB]
        w = jnp.where(u_edge, values[0], roll(values[1], half))
        w = roll(w, 2 * x)
        hit = jnp.logical_or(near_lane(x, 2 * x), near_lane(x, 2 * x + half))
        bl = b * SUB
        pk[k, bl : bl + SUB, :] = jnp.where(hit, w, pk[k, bl : bl + SUB, :])

    def put_diag(slot, k):
        for side, x in ((0, 1), (1, R)):
            acc = jnp.zeros((SUB, LANES), f32)
            for b in range(LB):
                lv = PAD + b * SUB
                u = U[slot, 0, x, lv : lv + SUB, :]
                v = U[slot, 1, x, lv : lv + SUB, :]
                w = jnp.where(u_edge, u, roll(v, half))
                w = roll(w, 2 * b) if b else w
                hit = jnp.logical_or(near_lane(b, 2 * b), near_lane(b, 2 * b + half))
                acc = jnp.where(hit, w, acc)
            dk[k, side] = acc

    def fill_level_pads(slot, row):
        for f in range(2):
            U[slot, f, row, PAD - 1 : PAD, :] = U[slot, f, row, PAD : PAD + 1, :]
            U[slot, f, row, PAD + L : PAD + L + 1, :] = U[
                slot, f, row, PAD + L - 1 : PAD + L, :
            ]

    def lane_parts(f, row, b, u, edge):
        up = roll(jnp.where(first, edge, u), LANES - 1)
        down = roll(jnp.where(last, edge, u), 1)
        bl = b * SUB
        DY[f, row, bl : bl + SUB, :] = up - down
        return up + down, bl

    def prepare(k):
        slot = k % 2
        for side, row in ((0, 0), (1, R + 1)):
            for f in range(2):
                U[slot, f, row, PAD : PAD + L, :] = row_rx[k, side, f]
            if k < SWEEPS:
                corner = jnp.where(odd, diag_rx[k, side, 0], diag_rx[k, side, 1])
                for b in range(LB):
                    lv = PAD + b * SUB
                    for f in range(2):
                        edge = roll(corner, (2 * LANES - 2 * b - f * half) % LANES)
                        lane_parts(f, row, b, U[slot, f, row, lv : lv + SUB, :], edge)

        def body(x, c):
            for b in range(LB):
                lv = PAD + b * SUB
                bl = b * SUB
                halo = jnp.where(
                    odd, col_rx[k, 0, bl : bl + SUB, :], col_rx[k, 1, bl : bl + SUB, :]
                )
                for f in range(2):
                    edge = roll(halo, back(x, f * half))
                    u = U[slot, f, x + 1, lv : lv + SUB, :]
                    s, _ = lane_parts(f, x + 1, b, u, edge)
                    if k < SWEEPS:
                        SY[f, x, bl : bl + SUB, :] = s
            return c

        lax.fori_loop(0, R, body, 0)

    def strain(slot, x, b):
        lv = PAD + b * SUB
        bl = b * SUB
        ue = U[slot, 0, x + 2, lv : lv + SUB, :]
        uw = U[slot, 0, x, lv : lv + SUB, :]
        ve = U[slot, 1, x + 2, lv : lv + SUB, :]
        vw = U[slot, 1, x, lv : lv + SUB, :]
        uu = U[slot, 0, x + 1, lv + 1 : lv + 1 + SUB, :]
        ul = U[slot, 0, x + 1, lv - 1 : lv - 1 + SUB, :]
        vu = U[slot, 1, x + 1, lv + 1 : lv + 1 + SUB, :]
        vl = U[slot, 1, x + 1, lv - 1 : lv - 1 + SUB, :]
        dyu = DY[0, x + 1, bl : bl + SUB, :]
        dyv = DY[1, x + 1, bl : bl + SUB, :]
        xx = ue - uw
        shear = dyu + (ve - vw)
        du = uu - ul
        dv = vu - vl
        effective = 0.25 * (
            xx * xx + dyv * dyv + xx * dyv + 0.25 * (shear * shear + du * du + dv * dv)
        )
        rate = Q[1, x, bl : bl + SUB, :]
        viscosity = rate * jnp.exp(jnp.log(effective + 0.01) * (-1.0 / 3.0))
        return effective, viscosity, ue + uw, ve + vw, uu + ul, vu + vl

    def sweep(k):
        slot = k % 2
        new_slot = (k + 1) % 2

        def body(x, c):
            ice = icy[pl.ds(x, 1), :].astype(f32)
            drag = slide[pl.ds(x, 1), :] * bed[pl.ds(x, 1), :].astype(f32)
            water = 1.0 - ice
            gu = grav[0, pl.ds(x, 1), :]
            gv = grav[1, pl.ds(x, 1), :]
            for b in range(LB):
                bl = b * SUB
                _, visc, sxu, sxv, szu, szv = strain(slot, x, b)
                diagonal = 22.0 * visc + water
                if b == 0:
                    diagonal = diagonal + jnp.where(subl == 0, drag, 0.0)
                cross_u = DY[1, x + 2, bl : bl + SUB, :] - DY[1, x, bl : bl + SUB, :]
                cross_v = DY[0, x + 2, bl : bl + SUB, :] - DY[0, x, bl : bl + SUB, :]
                near_u = 4.0 * (sxu + szu) + SY[0, x, bl : bl + SUB, :] + 0.75 * cross_u
                near_v = (
                    sxv + 4.0 * (SY[1, x, bl : bl + SUB, :] + szv) + 0.75 * cross_v
                )
                scale = ice / diagonal
                new_u = (gu + visc * near_u) * scale
                new_v = (gv + visc * near_v) * scale
                put_vel(new_slot, k + 1, x, b, (new_u, new_v))
                if k == SWEEPS - 1:
                    place = pl.ds(bl * R + x, SUB, stride=R)
                    vel_flat[0][place, :] = new_u
                    vel_flat[1][place, :] = new_v
            return c

        lax.fori_loop(0, R, body, 0)

    def th_moves(k):
        slot = k % 2
        return [
            ((1, 0), T.at[slot, R, PAD : PAD + L, :], trow_rx.at[k, 0]),
            ((-1, 0), T.at[slot, 1, PAD : PAD + L, :], trow_rx.at[k, 1]),
            ((0, 1), tpk.at[k], tcol_rx.at[k, 0]),
            ((0, -1), tpk.at[k], tcol_rx.at[k, 1]),
        ]

    def put_theta(slot, k, x, b, value):
        lv = PAD + b * SUB
        bl = b * SUB
        T[slot, x + 1, lv : lv + SUB, :] = value
        w = roll(value, 2 * x)
        tpk[k, bl : bl + SUB, :] = jnp.where(
            near_lane(x, 2 * x), w, tpk[k, bl : bl + SUB, :]
        )

    def section(k, x0, rows):
        slot = k % 2
        new_slot = (k + 1) % 2

        def body(i, c):
            x = x0 + i
            for b in range(LB):
                lv = PAD + b * SUB
                bl = b * SUB
                halo = jnp.where(
                    odd, tcol_rx[k, 0, bl : bl + SUB, :], tcol_rx[k, 1, bl : bl + SUB, :]
                )
                edge = roll(halo, back(x))
                center = T[slot, x + 1, lv : lv + SUB, :]
                north = roll(jnp.where(first, edge, center), LANES - 1)
                south = roll(jnp.where(last, edge, center), 1)
                east = T[slot, x + 2, lv : lv + SUB, :]
                west = T[slot, x, lv : lv + SUB, :]
                upper = T[slot, x + 1, lv + 1 : lv + 1 + SUB, :]
                lower = T[slot, x + 1, lv - 1 : lv - 1 + SUB, :]
                u = U[SWEEPS % 2, 0, x + 1, lv : lv + SUB, :]
                v = U[SWEEPS % 2, 1, x + 1, lv : lv + SUB, :]
                advect = (
                    jnp.maximum(u, 0.0) * (center - west)
                    + jnp.minimum(u, 0.0) * (east - center)
                    + jnp.maximum(v, 0.0) * (center - south)
                    + jnp.minimum(v, 0.0) * (north - center)
                )
                value = (
                    center
                    + 0.1 * (east + west + north + south - 4.0 * center)
                    + 0.2 * (upper + lower - 2.0 * center)
                    - 0.05 * advect
                    + Q[0, x, bl : bl + SUB, :]
                )
                if k < SECTIONS - 1:
                    put_theta(new_slot, k + 1, x, b, value)
                else:
                    place = pl.ds(bl * R + x, SUB, stride=R)
                    warm_flat[place, :] = value
                    hard_flat[place, :] = jnp.exp(-0.6 * value)
            return c

        lax.fori_loop(0, rows, body, 0)

    vel_flat = [vel_st.at[f].reshape(L * R, LANES) for f in range(2)]
    rate_flat = rate_st.reshape(L * R, LANES)
    warm_flat = warm_st.reshape(L * R, LANES)
    hard_flat = hard_st.reshape(L * R, LANES)

    for cp in vel_cp:
        cp.wait()

    def load_vel(x, c):
        for b in range(LB):
            place = pl.ds(b * SUB * R + x, SUB, stride=R)
            put_vel(0, 0, x, b, (vel_flat[0][place, :], vel_flat[1][place, :]))
        return c

    pk[...] = jnp.zeros_like(pk)
    tpk[...] = jnp.zeros_like(tpk)
    lax.fori_loop(0, R, load_vel, 0)
    put_diag(0, 0)
    start(vel_moves(0), vs_sem.at[0], vr_sem.at[0])
    warm = [warm_copy(d) for d in range(m)]
    for cp in warm:
        cp.start()
    rate_cp.wait()

    def load_rate(x, c):
        for b in range(LB):
            place = pl.ds(b * SUB * R + x, SUB, stride=R)
            Q[1, x, b * SUB : (b + 1) * SUB, :] = rate_flat[place, :]
        return c

    lax.fori_loop(0, R, load_rate, 0)

    for k in range(SWEEPS):
        finish(vel_moves(k), vs_sem.at[k], vr_sem.at[k])
        prepare(k)
        sweep(k)
        if k + 1 < SWEEPS:
            put_diag((k + 1) % 2, k + 1)
        start(vel_moves(k + 1), vs_sem.at[k + 1], vr_sem.at[k + 1])
        if k == 1:
            for cp in warm:
                cp.wait()
            for slot in range(2):
                for x in range(R + 2):
                    T[slot, x, PAD - 1 : PAD, :] = jnp.zeros((1, LANES), f32)
                    T[slot, x, PAD + L : PAD + L + 1, :] = jnp.zeros((1, LANES), f32)

            def load_warm(x, c):
                for b in range(LB):
                    place = pl.ds(b * SUB * R + x, SUB, stride=R)
                    put_theta(0, 0, x, b, warm_flat[place, :])
                return c

            lax.fori_loop(0, R, load_warm, 0)
            start(th_moves(0), ts_sem.at[0], tr_sem.at[0])

    vel_back = [
        pltpu.make_async_copy(vel_st.at[f], vel_out.at[f], loc_sem.at[f]) for f in range(2)
    ]
    for cp in vel_back:
        cp.start()

    finish(vel_moves(SWEEPS), vs_sem.at[SWEEPS], vr_sem.at[SWEEPS])
    prepare(SWEEPS)

    def heat_body(x, c):
        ice = icy[pl.ds(x, 1), :].astype(f32)
        for b in range(LB):
            bl = b * SUB
            effective, visc = strain(SWEEPS % 2, x, b)[:2]
            Q[0, x, bl : bl + SUB, :] = (ice * 0.1) * visc * effective
        return c

    lax.fori_loop(0, R, heat_body, 0)

    outs = []
    for k in range(SECTIONS):
        finish(th_moves(k), ts_sem.at[k], tr_sem.at[k])
        for side, row in ((0, 0), (1, R + 1)):
            T[k % 2, row, PAD : PAD + L, :] = trow_rx[k, side]
        if k < SECTIONS - 1:
            section(k, 0, R)
            start(th_moves(k + 1), ts_sem.at[k + 1], tr_sem.at[k + 1])
            continue
        for c in range(R // SUB):
            section(k, c * SUB, SUB)
            for d in list(range(1, m)) + [0]:
                to = lax.rem(g + d, m)
                src = warm_st.at[pl.ds(to * LG, LG), c * SUB : (c + 1) * SUB, :]
                dst = temp_out.at[
                    :,
                    c * SUB : (c + 1) * SUB,
                    pl.ds(pl.multiple_of(g * LANES, LANES), LANES),
                ]
                if d == 0:
                    cp = pltpu.make_async_copy(src, dst, os_sem.at[c, 0])
                else:
                    cp = pltpu.make_async_remote_copy(
                        src,
                        dst,
                        os_sem.at[c, d],
                        or_sem.at[c, d],
                        device_id=(t, to),
                        device_id_type=MESH,
                    )
                cp.start()
                outs.append(cp)
    hard_back = pltpu.make_async_copy(hard_st, hard_out, loc_sem.at[2])
    hard_back.start()
    for cp in outs:
        cp.wait()
    for cp in vel_back:
        cp.wait()
    hard_back.wait()


def local(n, m, vel, rate, warm, grav, slide, icy, bed):
    _, L, R, Y = vel.shape
    LG = L // m
    assert Y == LANES and 4 * R <= LANES and R % SUB == 0 and L % (SUB * m) == 0
    f32 = jnp.float32
    any_spec = pl.BlockSpec(memory_space=pl.ANY)
    vmem = pl.BlockSpec(memory_space=pltpu.VMEM)
    K = SWEEPS + 1
    V = pltpu.VMEM
    dma = pltpu.SemaphoreType.DMA
    return pl.pallas_call(
        functools.partial(kernel, n, m, R, L, LG),
        out_shape=(
            jax.ShapeDtypeStruct(vel.shape, f32),
            jax.ShapeDtypeStruct(warm.shape, f32),
            jax.ShapeDtypeStruct(rate.shape, f32),
        ),
        in_specs=[any_spec] * 3 + [vmem] * 4,
        out_specs=(any_spec,) * 3,
        scratch_shapes=[
            V((2, L, R, LANES), f32),
            V((L, R, LANES), f32),
            V((L, R, LANES), f32),
            V((L, R, LANES), f32),
            V((2, 2, R + 2, L + 2 * PAD, LANES), f32),
            V((2, R + 2, L, LANES), f32),
            V((2, R, L, LANES), f32),
            V((2, R + 2, L + 2 * PAD, LANES), f32),
            V((2, R, L, LANES), f32),
            V((K, L, LANES), f32),
            V((SWEEPS, 2, SUB, LANES), f32),
            V((K, 2, 2, L, LANES), f32),
            V((K, 2, L, LANES), f32),
            V((SWEEPS, 2, 2, SUB, LANES), f32),
            V((SECTIONS, L, LANES), f32),
            V((SECTIONS, 2, L, LANES), f32),
            V((SECTIONS, 2, L, LANES), f32),
            dma((4,)),
            dma((K, 8)),
            dma((K, 8)),
            dma((SECTIONS, 4)),
            dma((SECTIONS, 4)),
            dma((m,)),
            dma((m,)),
            dma((R // SUB, m)),
            dma((R // SUB, m)),
        ],
        compiler_params=pltpu.CompilerParams(
            collective_id=0, has_side_effects=True, vmem_limit_bytes=48 * 1024 * 1024
        ),
        name="ice_step",
    )(vel, rate, warm, grav, slide, icy, bed)


def solution(mesh):
    return jax.shard_map(
        functools.partial(local, mesh.shape["tile"], mesh.shape["grp"]),
        mesh=mesh,
        in_specs=(
            P(None, None, "tile", "grp"),
            P(None, "tile", "grp"),
            P("grp", "tile", None),
            P(None, "tile", "grp"),
            P("tile", "grp"),
            P("tile", "grp"),
            P("tile", "grp"),
        ),
        out_specs=(P(None, None, "tile", "grp"), P("grp", "tile", None), P(None, "tile", "grp")),
        check_vma=False,
    )
```

time: 380 us -> 164 us (0.43)
  the two profiles are of different devices: /device:TPU:2 before, /device:TPU:0 now
where the time goes in v1:
time: 164 us; the launch traced here: 163 us
  Pallas kernels  152 us (93%)
  local copies, waits for them, and re-layouts  10.4 us (6%)
    pallas_call x1, Pallas kernels, local(): pl.pallas_call(functools.partial(kernel, n, m, R, L, LG), out_shape=(jax....  152 us
    unnamed x15, local copies, waits for them, and re-layouts  10.4 us

profile of v1, /device:TPU:0, one launch (start us, length us, event | category | flops | bytes accessed | tf_op | source)
XLA Modules:
  0.0 162.8 jit_solution(15883924595820298411)
XLA Ops:
  0.6 0.0 copy-start
  0.6 1.2 copy-done
  1.9 0.0 copy-start.1
  1.9 1.2 copy-done.1
  3.1 0.0 copy-start.2
  3.1 0.8 copy-done.2
  3.8 0.0 copy-start.3
  3.8 0.7 copy-done.3
  4.6 0.0 copy-start.4
  4.6 0.7 copy-done.4
  5.3 0.0 copy-start.5
  5.3 0.7 copy-done.5
  6.0 151.8 %ice_step.1 = (f32[2,64,32,128]{3,2,1,0:T(8,128)}, f32[16,32,512]{2,1,0:T(8,128)S(1)}, f32[64,32,128]{2,1,0:T(8,128)S(1)}) custom-call(f32[2,64,32,128]{3,2,1,0:T(8,128)} %vel_in.1, f32[64,32,128]{2,1,0:T(8,128)S(1)} %copy-done, f32[16,32,512]{2,1,0:T(8,128)S(1)} %copy-done.1, f32[2,32,128]{2,1,0:T(8,128)S(1)} %copy-done.2, f32[32,128]{1,0:T(8,128)S(1)} %copy-done.3, ...), custom_call_target="tpu_custom_call" | custom-call | tf_op jit(solution)/shard_map/ice_step/pallas_call | solution.py:510
  157.8 3.1 %copy.13 = f32[2,64,32,128]{3,2,1,0:T(8,128)} copy(f32[2,64,32,128]{3,2,1,0:T(8,128)} %get-tuple-element.6) | data formatting | bytes 4194304
  160.8 1.0 copy.14
  161.8 1.0 copy.15
Async XLA Ops:
  0.6 1.2 copy-start
  1.9 1.2 copy-start.1
  3.1 0.8 copy-start.2
  3.8 0.7 copy-start.3
  4.6 0.7 copy-start.4
  5.3 0.7 copy-start.5

commit v2 on v1

--- a/solution.py
+++ b/solution.py
@@ -40,10 +40,14 @@
     rate_st,
     warm_st,
     hard_st,
-    U,
+    U0,
+    U1,
     DY,
     SY,
-    T,
+    T0,
+    T1,
+    mh,
+    tmh,
     Q,
     pk,
     dk,
@@ -66,6 +70,9 @@
     t = lax.axis_index("tile")
     g = lax.axis_index("grp")
     LB = L // SUB
+    U = (U0, U1)
+    T = (T0, T1)
+    STEP = 2
     f32 = jnp.float32
 
     vel_cp = [
@@ -127,7 +134,7 @@
     u_edge = jnp.logical_or(first, last)
 
     def back(x, extra=0):
-        return lax.rem(2 * LANES - 2 * x - extra, LANES)
+        return lax.rem(2 * LANES - 1 - 2 * x - extra, LANES)
 
     def near_lane(x, shift):
         lane_x = lax.rem(lane + (LANES + 1) - shift, LANES)
@@ -136,8 +143,8 @@
     def vel_moves(k):
         slot = k % 2
         moves = [
-            ((1, 0), U.at[slot, :, R, PAD : PAD + L, :], row_rx.at[k, 0]),
-            ((-1, 0), U.at[slot, :, 1, PAD : PAD + L, :], row_rx.at[k, 1]),
+            ((1, 0), U[slot].at[:, R, PAD : PAD + L, :], row_rx.at[k, 0]),
+            ((-1, 0), U[slot].at[:, 1, PAD : PAD + L, :], row_rx.at[k, 1]),
             ((0, 1), pk.at[k], col_rx.at[k, 0]),
             ((0, -1), pk.at[k], col_rx.at[k, 1]),
         ]
@@ -192,24 +199,26 @@
     def put_vel(slot, k, x, b, values):
         lv = PAD + b * SUB
         for f in range(2):
-            U[slot, f, x + 1, lv : lv + SUB, :] = values[f]
+            U[slot][f, x + 1, lv : lv + SUB, :] = values[f]
             if b == 0:
-                U[slot, f, x + 1, lv - 1 : lv, :] = values[f][0:1]
+                U[slot][f, x + 1, lv - 1 : lv, :] = values[f][0:1]
             if b == LB - 1:
-                U[slot, f, x + 1, lv + SUB : lv + SUB + 1, :] = values[f][SUB - 1 : SUB]
-        w = jnp.where(u_edge, values[0], roll(values[1], half))
-        w = roll(w, 2 * x)
-        hit = jnp.logical_or(near_lane(x, 2 * x), near_lane(x, 2 * x + half))
+                U[slot][f, x + 1, lv + SUB : lv + SUB + 1, :] = values[f][SUB - 1 : SUB]
         bl = b * SUB
-        pk[k, bl : bl + SUB, :] = jnp.where(hit, w, pk[k, bl : bl + SUB, :])
+        w = jnp.where(
+            near_lane(x, 2 * x + half),
+            roll(values[1], lax.rem(2 * x + half, LANES)),
+            pk[k, bl : bl + SUB, :],
+        )
+        pk[k, bl : bl + SUB, :] = jnp.where(near_lane(x, 2 * x), roll(values[0], 2 * x), w)
 
     def put_diag(slot, k):
         for side, x in ((0, 1), (1, R)):
             acc = jnp.zeros((SUB, LANES), f32)
             for b in range(LB):
                 lv = PAD + b * SUB
-                u = U[slot, 0, x, lv : lv + SUB, :]
-                v = U[slot, 1, x, lv : lv + SUB, :]
+                u = U[slot][0, x, lv : lv + SUB, :]
+                v = U[slot][1, x, lv : lv + SUB, :]
                 w = jnp.where(u_edge, u, roll(v, half))
                 w = roll(w, 2 * b) if b else w
                 hit = jnp.logical_or(near_lane(b, 2 * b), near_lane(b, 2 * b + half))
@@ -218,14 +227,14 @@
 
     def fill_level_pads(slot, row):
         for f in range(2):
-            U[slot, f, row, PAD - 1 : PAD, :] = U[slot, f, row, PAD : PAD + 1, :]
-            U[slot, f, row, PAD + L : PAD + L + 1, :] = U[
-                slot, f, row, PAD + L - 1 : PAD + L, :
+            U[slot][f, row, PAD - 1 : PAD, :] = U[slot][f, row, PAD : PAD + 1, :]
+            U[slot][f, row, PAD + L : PAD + L + 1, :] = U[slot][
+                f, row, PAD + L - 1 : PAD + L, :
             ]
 
     def lane_parts(f, row, b, u, edge):
-        up = roll(jnp.where(first, edge, u), LANES - 1)
-        down = roll(jnp.where(last, edge, u), 1)
+        up = jnp.where(last, edge, roll(u, LANES - 1))
+        down = jnp.where(first, edge, roll(u, 1))
         bl = b * SUB
         DY[f, row, bl : bl + SUB, :] = up - down
         return up + down, bl
@@ -234,43 +243,48 @@
         slot = k % 2
         for side, row in ((0, 0), (1, R + 1)):
             for f in range(2):
-                U[slot, f, row, PAD : PAD + L, :] = row_rx[k, side, f]
+                U[slot][f, row, PAD : PAD + L, :] = row_rx[k, side, f]
             if k < SWEEPS:
-                corner = jnp.where(odd, diag_rx[k, side, 0], diag_rx[k, side, 1])
+                corner = jnp.where(odd, roll(diag_rx[k, side, 0], 2), diag_rx[k, side, 1])
                 for b in range(LB):
                     lv = PAD + b * SUB
                     for f in range(2):
-                        edge = roll(corner, (2 * LANES - 2 * b - f * half) % LANES)
-                        lane_parts(f, row, b, U[slot, f, row, lv : lv + SUB, :], edge)
-
-        def body(x, c):
+                        edge = roll(corner, (2 * LANES - 2 * b - 1 - f * half) % LANES)
+                        lane_parts(f, row, b, U[slot][f, row, lv : lv + SUB, :], edge)
+
+        for b in range(LB):
+            bl = b * SUB
+            mh[bl : bl + SUB, :] = jnp.where(
+                odd, roll(col_rx[k, 0, bl : bl + SUB, :], 2), col_rx[k, 1, bl : bl + SUB, :]
+            )
+
+        def body(i, c):
             for b in range(LB):
                 lv = PAD + b * SUB
                 bl = b * SUB
-                halo = jnp.where(
-                    odd, col_rx[k, 0, bl : bl + SUB, :], col_rx[k, 1, bl : bl + SUB, :]
-                )
-                for f in range(2):
-                    edge = roll(halo, back(x, f * half))
-                    u = U[slot, f, x + 1, lv : lv + SUB, :]
-                    s, _ = lane_parts(f, x + 1, b, u, edge)
-                    if k < SWEEPS:
-                        SY[f, x, bl : bl + SUB, :] = s
+                halo = mh[bl : bl + SUB, :]
+                for x in [i * STEP + j for j in range(STEP)]:
+                    for f in range(2):
+                        edge = roll(halo, back(x, f * half))
+                        u = U[slot][f, x + 1, lv : lv + SUB, :]
+                        s, _ = lane_parts(f, x + 1, b, u, edge)
+                        if k < SWEEPS:
+                            SY[f, x, bl : bl + SUB, :] = s
             return c
 
-        lax.fori_loop(0, R, body, 0)
+        lax.fori_loop(0, R // STEP, body, 0)
 
     def strain(slot, x, b):
         lv = PAD + b * SUB
         bl = b * SUB
-        ue = U[slot, 0, x + 2, lv : lv + SUB, :]
-        uw = U[slot, 0, x, lv : lv + SUB, :]
-        ve = U[slot, 1, x + 2, lv : lv + SUB, :]
-        vw = U[slot, 1, x, lv : lv + SUB, :]
-        uu = U[slot, 0, x + 1, lv + 1 : lv + 1 + SUB, :]
-        ul = U[slot, 0, x + 1, lv - 1 : lv - 1 + SUB, :]
-        vu = U[slot, 1, x + 1, lv + 1 : lv + 1 + SUB, :]
-        vl = U[slot, 1, x + 1, lv - 1 : lv - 1 + SUB, :]
+        ue = U[slot][0, x + 2, lv : lv + SUB, :]
+        uw = U[slot][0, x, lv : lv + SUB, :]
+        ve = U[slot][1, x + 2, lv : lv + SUB, :]
+        vw = U[slot][1, x, lv : lv + SUB, :]
+        uu = U[slot][0, x + 1, lv + 1 : lv + 1 + SUB, :]
+        ul = U[slot][0, x + 1, lv - 1 : lv - 1 + SUB, :]
+        vu = U[slot][1, x + 1, lv + 1 : lv + 1 + SUB, :]
+        vl = U[slot][1, x + 1, lv - 1 : lv - 1 + SUB, :]
         dyu = DY[0, x + 1, bl : bl + SUB, :]
         dyv = DY[1, x + 1, bl : bl + SUB, :]
         xx = ue - uw
@@ -288,7 +302,7 @@
         slot = k % 2
         new_slot = (k + 1) % 2
 
-        def body(x, c):
+        def row(x):
             ice = icy[pl.ds(x, 1), :].astype(f32)
             drag = slide[pl.ds(x, 1), :] * bed[pl.ds(x, 1), :].astype(f32)
             water = 1.0 - ice
@@ -314,15 +328,19 @@
                     place = pl.ds(bl * R + x, SUB, stride=R)
                     vel_flat[0][place, :] = new_u
                     vel_flat[1][place, :] = new_v
+
+        def body(i, c):
+            for j in range(STEP):
+                row(i * STEP + j)
             return c
 
-        lax.fori_loop(0, R, body, 0)
+        lax.fori_loop(0, R // STEP, body, 0)
 
     def th_moves(k):
         slot = k % 2
         return [
-            ((1, 0), T.at[slot, R, PAD : PAD + L, :], trow_rx.at[k, 0]),
-            ((-1, 0), T.at[slot, 1, PAD : PAD + L, :], trow_rx.at[k, 1]),
+            ((1, 0), T[slot].at[R, PAD : PAD + L, :], trow_rx.at[k, 0]),
+            ((-1, 0), T[slot].at[1, PAD : PAD + L, :], trow_rx.at[k, 1]),
             ((0, 1), tpk.at[k], tcol_rx.at[k, 0]),
             ((0, -1), tpk.at[k], tcol_rx.at[k, 1]),
         ]
@@ -330,7 +348,7 @@
     def put_theta(slot, k, x, b, value):
         lv = PAD + b * SUB
         bl = b * SUB
-        T[slot, x + 1, lv : lv + SUB, :] = value
+        T[slot][x + 1, lv : lv + SUB, :] = value
         w = roll(value, 2 * x)
         tpk[k, bl : bl + SUB, :] = jnp.where(
             near_lane(x, 2 * x), w, tpk[k, bl : bl + SUB, :]
@@ -340,24 +358,20 @@
         slot = k % 2
         new_slot = (k + 1) % 2
 
-        def body(i, c):
-            x = x0 + i
+        def row(x):
             for b in range(LB):
                 lv = PAD + b * SUB
                 bl = b * SUB
-                halo = jnp.where(
-                    odd, tcol_rx[k, 0, bl : bl + SUB, :], tcol_rx[k, 1, bl : bl + SUB, :]
-                )
-                edge = roll(halo, back(x))
-                center = T[slot, x + 1, lv : lv + SUB, :]
-                north = roll(jnp.where(first, edge, center), LANES - 1)
-                south = roll(jnp.where(last, edge, center), 1)
-                east = T[slot, x + 2, lv : lv + SUB, :]
-                west = T[slot, x, lv : lv + SUB, :]
-                upper = T[slot, x + 1, lv + 1 : lv + 1 + SUB, :]
-                lower = T[slot, x + 1, lv - 1 : lv - 1 + SUB, :]
-                u = U[SWEEPS % 2, 0, x + 1, lv : lv + SUB, :]
-                v = U[SWEEPS % 2, 1, x + 1, lv : lv + SUB, :]
+                edge = roll(tmh[bl : bl + SUB, :], back(x))
+                center = T[slot][x + 1, lv : lv + SUB, :]
+                north = jnp.where(last, edge, roll(center, LANES - 1))
+                south = jnp.where(first, edge, roll(center, 1))
+                east = T[slot][x + 2, lv : lv + SUB, :]
+                west = T[slot][x, lv : lv + SUB, :]
+                upper = T[slot][x + 1, lv + 1 : lv + 1 + SUB, :]
+                lower = T[slot][x + 1, lv - 1 : lv - 1 + SUB, :]
+                u = U[SWEEPS % 2][0, x + 1, lv : lv + SUB, :]
+                v = U[SWEEPS % 2][1, x + 1, lv : lv + SUB, :]
                 advect = (
                     jnp.maximum(u, 0.0) * (center - west)
                     + jnp.minimum(u, 0.0) * (east - center)
@@ -377,9 +391,13 @@
                     place = pl.ds(bl * R + x, SUB, stride=R)
                     warm_flat[place, :] = value
                     hard_flat[place, :] = jnp.exp(-0.6 * value)
+
+        def body(i, c):
+            for j in range(STEP):
+                row(x0 + i * STEP + j)
             return c
 
-        lax.fori_loop(0, rows, body, 0)
+        lax.fori_loop(0, rows // STEP, body, 0)
 
     vel_flat = [vel_st.at[f].reshape(L * R, LANES) for f in range(2)]
     rate_flat = rate_st.reshape(L * R, LANES)
@@ -401,8 +419,7 @@
     put_diag(0, 0)
     start(vel_moves(0), vs_sem.at[0], vr_sem.at[0])
     warm = [warm_copy(d) for d in range(m)]
-    for cp in warm:
-        cp.start()
+    warm[0].start()
     rate_cp.wait()
 
     def load_rate(x, c):
@@ -415,18 +432,20 @@
 
     for k in range(SWEEPS):
         finish(vel_moves(k), vs_sem.at[k], vr_sem.at[k])
+        for cp in warm[1 + k :] if k == SWEEPS - 1 else warm[1 + k : 2 + k]:
+            cp.start()
         prepare(k)
         sweep(k)
         if k + 1 < SWEEPS:
             put_diag((k + 1) % 2, k + 1)
         start(vel_moves(k + 1), vs_sem.at[k + 1], vr_sem.at[k + 1])
-        if k == 1:
+        if k == SWEEPS - 1:
             for cp in warm:
                 cp.wait()
             for slot in range(2):
                 for x in range(R + 2):
-                    T[slot, x, PAD - 1 : PAD, :] = jnp.zeros((1, LANES), f32)
-                    T[slot, x, PAD + L : PAD + L + 1, :] = jnp.zeros((1, LANES), f32)
+                    T[slot][x, PAD - 1 : PAD, :] = jnp.zeros((1, LANES), f32)
+                    T[slot][x, PAD + L : PAD + L + 1, :] = jnp.zeros((1, LANES), f32)
 
             def load_warm(x, c):
                 for b in range(LB):
@@ -446,21 +465,30 @@
     finish(vel_moves(SWEEPS), vs_sem.at[SWEEPS], vr_sem.at[SWEEPS])
     prepare(SWEEPS)
 
-    def heat_body(x, c):
+    def heat_row(x):
         ice = icy[pl.ds(x, 1), :].astype(f32)
         for b in range(LB):
             bl = b * SUB
             effective, visc = strain(SWEEPS % 2, x, b)[:2]
             Q[0, x, bl : bl + SUB, :] = (ice * 0.1) * visc * effective
+
+    def heat_body(i, c):
+        for j in range(STEP):
+            heat_row(i * STEP + j)
         return c
 
-    lax.fori_loop(0, R, heat_body, 0)
+    lax.fori_loop(0, R // STEP, heat_body, 0)
 
     outs = []
     for k in range(SECTIONS):
         finish(th_moves(k), ts_sem.at[k], tr_sem.at[k])
         for side, row in ((0, 0), (1, R + 1)):
-            T[k % 2, row, PAD : PAD + L, :] = trow_rx[k, side]
+            T[k % 2][row, PAD : PAD + L, :] = trow_rx[k, side]
+        for b in range(LB):
+            bl = b * SUB
+            tmh[bl : bl + SUB, :] = jnp.where(
+                odd, roll(tcol_rx[k, 0, bl : bl + SUB, :], 2), tcol_rx[k, 1, bl : bl + SUB, :]
+            )
         if k < SECTIONS - 1:
             section(k, 0, R)
             start(th_moves(k + 1), ts_sem.at[k + 1], tr_sem.at[k + 1])
@@ -521,10 +549,14 @@
             V((L, R, LANES), f32),
             V((L, R, LANES), f32),
             V((L, R, LANES), f32),
-            V((2, 2, R + 2, L + 2 * PAD, LANES), f32),
+            V((2, R + 2, L + 2 * PAD, LANES), f32),
+            V((2, R + 2, L + 2 * PAD, LANES), f32),
             V((2, R + 2, L, LANES), f32),
             V((2, R, L, LANES), f32),
-            V((2, R + 2, L + 2 * PAD, LANES), f32),
+            V((R + 2, L + 2 * PAD, LANES), f32),
+            V((R + 2, L + 2 * PAD, LANES), f32),
+            V((L, LANES), f32),
+            V((L, LANES), f32),
             V((2, R, L, LANES), f32),
             V((K, L, LANES), f32),
             V((SWEEPS, 2, SUB, LANES), f32),

time: 164 us -> 119 us (0.73)
  Pallas kernels: 152 us -> 107 us
    pallas_call x1, Pallas kernels: 152 us -> 107 us  [local(): pl.pallas_call(functools.partial(kernel, n, m, R, L, LG), out_shape=(jax....]
where the time goes in v2:
time: 119 us; the launch traced here: 118 us
  Pallas kernels  107 us (90%)
  local copies, waits for them, and re-layouts  10.4 us (9%)
    pallas_call x1, Pallas kernels, local(): pl.pallas_call(functools.partial(kernel, n, m, R, L, LG), out_shape=(jax....  107 us
    unnamed x15, local copies, waits for them, and re-layouts  10.4 us

profile of v2, /device:TPU:0, one launch (start us, length us, event | category | flops | bytes accessed | tf_op | source)
XLA Modules:
  0.0 118.3 jit_solution(3648256818950134917)
XLA Ops:
  0.6 0.0 copy-start
  0.6 1.2 %copy-done = f32[64,32,128]{2,1,0:T(8,128)S(1)} copy-done((f32[64,32,128]{2,1,0:T(8,128)S(1)}, f32[64,32,128]{2,1,0:T(8,128)}, u32[]{:S(2)}) %copy-start) | copy-done | bytes 1048600
  1.9 0.0 copy-start.1
  1.9 1.2 %copy-done.1 = f32[16,32,512]{2,1,0:T(8,128)S(1)} copy-done((f32[16,32,512]{2,1,0:T(8,128)S(1)}, f32[16,32,512]{2,1,0:T(8,128)}, u32[]{:S(2)}) %copy-start.1) | copy-done | bytes 1048600
  3.1 0.0 copy-start.2
  3.1 0.8 copy-done.2
  3.8 0.0 copy-start.3
  3.8 0.7 copy-done.3
  4.6 0.0 copy-start.4
  4.6 0.7 copy-done.4
  5.3 0.0 copy-start.5
  5.3 0.7 copy-done.5
  6.0 107.3 %ice_step.1 = (f32[2,64,32,128]{3,2,1,0:T(8,128)}, f32[16,32,512]{2,1,0:T(8,128)S(1)}, f32[64,32,128]{2,1,0:T(8,128)S(1)}) custom-call(f32[2,64,32,128]{3,2,1,0:T(8,128)} %vel_in.1, f32[64,32,128]{2,1,0:T(8,128)S(1)} %copy-done, f32[16,32,512]{2,1,0:T(8,128)S(1)} %copy-done.1, f32[2,32,128]{2,1,0:T(8,128)S(1)} %copy-done.2, f32[32,128]{1,0:T(8,128)S(1)} %copy-done.3, ...), custom_call_target="tpu_custom_call" | custom-call | tf_op jit(solution)/shard_map/ice_step/pallas_call | solution.py:538
  113.3 3.1 %copy.13 = f32[2,64,32,128]{3,2,1,0:T(8,128)} copy(f32[2,64,32,128]{3,2,1,0:T(8,128)} %get-tuple-element.6) | data formatting | bytes 4194304
  116.3 1.0 copy.14
  117.3 1.0 copy.15
Async XLA Ops:
  0.6 1.2 %copy-start = (f32[64,32,128]{2,1,0:T(8,128)S(1)}, f32[64,32,128]{2,1,0:T(8,128)}, u32[]{:S(2)}) copy-start(f32[64,32,128]{2,1,0:T(8,128)} %rate_in.1) | copy-start | bytes 3145732
  1.9 1.2 %copy-start.1 = (f32[16,32,512]{2,1,0:T(8,128)S(1)}, f32[16,32,512]{2,1,0:T(8,128)}, u32[]{:S(2)}) copy-start(f32[16,32,512]{2,1,0:T(8,128)} %warm_in.1) | copy-start | bytes 3145732
  3.1 0.8 copy-start.2
  3.8 0.7 copy-start.3
  4.6 0.7 copy-start.4
  5.3 0.7 copy-start.5

commit v3 on v2

--- a/solution.py
+++ b/solution.py
@@ -157,8 +157,10 @@
             ]
         return moves
 
-    def start(moves, s_sem, r_sem):
+    def start(moves, s_sem, r_sem, early=None):
         for j, ((dt, dg), src, dst) in enumerate(moves):
+            if early is not None and early != (dt != 0):
+                continue
 
             @pl.when(has(dt, dg))
             def _(j=j, dt=dt, dg=dg, src=src, dst=dst):
@@ -330,11 +332,17 @@
                     vel_flat[1][place, :] = new_v
 
         def body(i, c):
-            for j in range(STEP):
-                row(i * STEP + j)
+            row(i)
+            row(R - 1 - i)
             return c
 
-        lax.fori_loop(0, R // STEP, body, 0)
+        lax.fori_loop(0, 1, body, 0)
+        if k + 1 < SWEEPS:
+            put_diag(new_slot, k + 1)
+        moves = vel_moves(k + 1), vs_sem.at[k + 1], vr_sem.at[k + 1]
+        start(*moves, early=True)
+        lax.fori_loop(1, R // 2, body, 0)
+        start(*moves, early=False)
 
     def th_moves(k):
         slot = k % 2
@@ -392,12 +400,26 @@
                     warm_flat[place, :] = value
                     hard_flat[place, :] = jnp.exp(-0.6 * value)
 
+        if k == SECTIONS - 1:
+
+            def chunk(i, c):
+                for j in range(STEP):
+                    row(x0 + i * STEP + j)
+                return c
+
+            lax.fori_loop(0, rows // STEP, chunk, 0)
+            return
+
         def body(i, c):
-            for j in range(STEP):
-                row(x0 + i * STEP + j)
+            row(i)
+            row(R - 1 - i)
             return c
 
-        lax.fori_loop(0, rows // STEP, body, 0)
+        lax.fori_loop(0, 1, body, 0)
+        moves = th_moves(k + 1), ts_sem.at[k + 1], tr_sem.at[k + 1]
+        start(*moves, early=True)
+        lax.fori_loop(1, R // 2, body, 0)
+        start(*moves, early=False)
 
     vel_flat = [vel_st.at[f].reshape(L * R, LANES) for f in range(2)]
     rate_flat = rate_st.reshape(L * R, LANES)
@@ -436,9 +458,6 @@
             cp.start()
         prepare(k)
         sweep(k)
-        if k + 1 < SWEEPS:
-            put_diag((k + 1) % 2, k + 1)
-        start(vel_moves(k + 1), vs_sem.at[k + 1], vr_sem.at[k + 1])
         if k == SWEEPS - 1:
             for cp in warm:
                 cp.wait()
@@ -491,7 +510,6 @@
             )
         if k < SECTIONS - 1:
             section(k, 0, R)
-            start(th_moves(k + 1), ts_sem.at[k + 1], tr_sem.at[k + 1])
             continue
         for c in range(R // SUB):
             section(k, c * SUB, SUB)
@@ -577,7 +595,7 @@
             dma((R // SUB, m)),
         ],
         compiler_params=pltpu.CompilerParams(
-            collective_id=0, has_side_effects=True, vmem_limit_bytes=48 * 1024 * 1024
+            collective_id=0, has_side_effects=True, vmem_limit_bytes=60 * 1024 * 1024
         ),
         name="ice_step",
     )(vel, rate, warm, grav, slide, icy, bed)

time: 119 us -> 112 us (0.941)
  local copies, waits for them, and re-layouts: 10.4 us -> 5.17 us
    unnamed x15 -> x7, local copies, waits for them, and re-layouts: 10.4 us -> 5.17 us
    pallas_call x1, Pallas kernels: 107 us -> 106 us  [local(): pl.pallas_call(functools.partial(kernel, n, m, R, L, LG), out_shape=(jax....]
where the time goes in v3:
time: 112 us; the launch traced here: 111 us
  Pallas kernels  106 us (95%)
  local copies, waits for them, and re-layouts  5.17 us (5%)
    pallas_call x1, Pallas kernels, local(): pl.pallas_call(functools.partial(kernel, n, m, R, L, LG), out_shape=(jax....  106 us
    unnamed x7, local copies, waits for them, and re-layouts  5.17 us

profile of v3, /device:TPU:0, one launch (start us, length us, event | category | flops | bytes accessed | tf_op | source)
XLA Modules:
  0.0 111.4 jit_solution(9751463015644662547)
XLA Ops:
  0.6 105.6 %ice_step.1 = (f32[2,64,32,128]{3,2,1,0:T(8,128)}, f32[16,32,512]{2,1,0:T(8,128)}, f32[64,32,128]{2,1,0:T(8,128)}) custom-call(f32[2,64,32,128]{3,2,1,0:T(8,128)} %vel_in.1, f32[64,32,128]{2,1,0:T(8,128)} %rate_in.1, f32[16,32,512]{2,1,0:T(8,128)} %warm_in.1, f32[2,32,128]{2,1,0:T(8,128)} %grav.1, f32[32,128]{1,0:T(8,128)} %slide.1, s32[32,128]{1,0:T(8,128)} %icy.1, ...), custom_call_target="tpu_custom_call" | custom-call | tf_op jit(solution)/shard_map/ice_step/pallas_call | solution.py:556
  106.2 0.0 copy-start.1
  106.3 0.0 copy-start
  106.3 3.2 %copy.13 = f32[2,64,32,128]{3,2,1,0:T(8,128)} copy(f32[2,64,32,128]{3,2,1,0:T(8,128)} %get-tuple-element.6) | data formatting | bytes 4194304
  109.5 0.0 copy-done.1
  109.5 1.0 copy.14
  110.5 0.0 copy-done
  110.5 1.0 copy.15
Async XLA Ops:
  106.2 3.2 %copy-start.1 = (f32[16,32,512]{2,1,0:T(8,128)S(1)}, f32[16,32,512]{2,1,0:T(8,128)}, u32[]{:S(2)}) copy-start(f32[16,32,512]{2,1,0:T(8,128)} %get-tuple-element.7) | copy-start | bytes 3145732
  106.3 4.2 %copy-start = (f32[64,32,128]{2,1,0:T(8,128)S(1)}, f32[64,32,128]{2,1,0:T(8,128)}, u32[]{:S(2)}) copy-start(f32[64,32,128]{2,1,0:T(8,128)} %get-tuple-element.8) | copy-start | bytes 3145732

commit v4 on v3

--- a/solution.py
+++ b/solution.py
@@ -73,6 +73,7 @@
     U = (U0, U1)
     T = (T0, T1)
     STEP = 2
+    WIDE = 4
     f32 = jnp.float32
 
     vel_cp = [
@@ -265,7 +266,7 @@
                 lv = PAD + b * SUB
                 bl = b * SUB
                 halo = mh[bl : bl + SUB, :]
-                for x in [i * STEP + j for j in range(STEP)]:
+                for x in [i * WIDE + j for j in range(WIDE)]:
                     for f in range(2):
                         edge = roll(halo, back(x, f * half))
                         u = U[slot][f, x + 1, lv : lv + SUB, :]
@@ -274,7 +275,7 @@
                             SY[f, x, bl : bl + SUB, :] = s
             return c
 
-        lax.fori_loop(0, R // STEP, body, 0)
+        lax.fori_loop(0, R // WIDE, body, 0)
 
     def strain(slot, x, b):
         lv = PAD + b * SUB
@@ -513,7 +514,7 @@
             continue
         for c in range(R // SUB):
             section(k, c * SUB, SUB)
-            for d in list(range(1, m)) + [0]:
+            for d in sorted(range(1, m), key=lambda d: -min(d, m - d)) + [0]:
                 to = lax.rem(g + d, m)
                 src = warm_st.at[pl.ds(to * LG, LG), c * SUB : (c + 1) * SUB, :]
                 dst = temp_out.at[

time: 112 us -> 112 us (level)
  no operation moved by 1% of the time
where the time goes in v4:
time: 112 us; the launch traced here: 111 us
  Pallas kernels  106 us (95%)
  local copies, waits for them, and re-layouts  5.17 us (5%)
    pallas_call x1, Pallas kernels, local(): pl.pallas_call(functools.partial(kernel, n, m, R, L, LG), out_shape=(jax....  106 us
    unnamed x7, local copies, waits for them, and re-layouts  5.17 us

profile of v4, /device:TPU:0, one launch (start us, length us, event | category | flops | bytes accessed | tf_op | source)
XLA Modules:
  0.0 111.5 jit_solution(8454560069124372999)
XLA Ops:
  0.6 105.6 %ice_step.1 = (f32[2,64,32,128]{3,2,1,0:T(8,128)}, f32[16,32,512]{2,1,0:T(8,128)}, f32[64,32,128]{2,1,0:T(8,128)}) custom-call(f32[2,64,32,128]{3,2,1,0:T(8,128)} %vel_in.1, f32[64,32,128]{2,1,0:T(8,128)} %rate_in.1, f32[16,32,512]{2,1,0:T(8,128)} %warm_in.1, f32[2,32,128]{2,1,0:T(8,128)} %grav.1, f32[32,128]{1,0:T(8,128)} %slide.1, s32[32,128]{1,0:T(8,128)} %icy.1, ...), custom_call_target="tpu_custom_call" | custom-call | tf_op jit(solution)/shard_map/ice_step/pallas_call | solution.py:557
  106.3 0.0 copy-start.1
  106.3 0.0 copy-start
  106.3 3.2 %copy.13 = f32[2,64,32,128]{3,2,1,0:T(8,128)} copy(f32[2,64,32,128]{3,2,1,0:T(8,128)} %get-tuple-element.6) | data formatting | bytes 4194304
  109.5 0.0 copy-done.1
  109.5 1.0 copy.14
  110.5 0.0 copy-done
  110.5 1.0 copy.15
Async XLA Ops:
  106.3 3.2 %copy-start.1 = (f32[16,32,512]{2,1,0:T(8,128)S(1)}, f32[16,32,512]{2,1,0:T(8,128)}, u32[]{:S(2)}) copy-start(f32[16,32,512]{2,1,0:T(8,128)} %get-tuple-element.7) | copy-start | bytes 3145732
  106.3 4.2 %copy-start = (f32[64,32,128]{2,1,0:T(8,128)S(1)}, f32[64,32,128]{2,1,0:T(8,128)}, u32[]{:S(2)}) copy-start(f32[64,32,128]{2,1,0:T(8,128)} %get-tuple-element.8) | copy-start | bytes 3145732
